TPU v7x, 512 devices: a whole 4x8x8 slice. The times are simulated.
512 devices in a mesh: rep: 4 (over z_hi), dp: 16 (over y, core), tensor: 8 (over x, z_lo).
Axes of the slice: x: 4, y: 8, z: 8 (z_hi: 4, z_lo: 2; z = z_hi * 2 + z_lo), core: 2. Of those that a mesh axis runs over, the one named last changes fastest.
Arguments:
- grad_proj: float32 [64, 3072, 1536], P(('rep', 'dp'), 'tensor'), as said below
- grad_conv: float32 [64, 4, 3328], P(('rep', 'dp'), None, 'tensor'), may hold values from -24 to 24
- param_proj: float32 [3072, 1536], P('tensor', 'dp'), may hold values from -6 to 6
- m_proj: float32 [3072, 1536], P('tensor', 'dp'), may hold values from -2 to 2
- v_proj: float32 [3072, 1536], P('tensor', 'dp'), may hold values from 0.02 to 0.2
- ema_proj: float32 [3072, 1536], P(('tensor', 'dp')), may hold values from -6 to 6
- param_conv: float32 [4, 3328], P(None, 'tensor'), may hold values from -3 to 3
- m_conv: float32 [4, 3328], P(None, 'tensor'), may hold values from -2 to 2
- v_conv: float32 [4, 3328], P(None, 'tensor'), may hold values from 0.02 to 0.2
Outputs:
- new_param_proj: float32 [3072, 1536], P('tensor', 'dp')
- new_m_proj: float32 [3072, 1536], P('tensor', 'dp')
- new_v_proj: float32 [3072, 1536], P('tensor', 'dp')
- new_ema_proj: float32 [3072, 1536], P(('tensor', 'dp'))
- weights_proj: bfloat16 [3072, 1536], P('tensor')
- new_param_conv: float32 [4, 3328], P(None, 'tensor')
- new_m_conv: float32 [4, 3328], P(None, 'tensor')
- new_v_conv: float32 [4, 3328], P(None, 'tensor')
Inputs may be any that keep to these rules, and one draw needn't show every extreme that they name: `grad_proj`: Real-valued gradients with entries of magnitude below 3100.
All inputs are finite; a program needn't handle non-finite values.
Results may differ from a plain program's by a relative error of at most 0.001.
Values may be sent and summed in bfloat16 or wider, within the bound.
A program may use at most 64 MiB of HBM per device.

v0:
```python
import math

import jax
import jax.numpy as jnp
from jax import lax
from jax.sharding import PartitionSpec as P

D = 1536
INNER = 3072
CONV = 3328
KCONV = 4


def adamw_step(param_in, first_in, second_in, grad_in):
    first_out = 0.9 * first_in + 0.1 * grad_in
    second_out = 0.95 * second_in + 0.05 * grad_in * grad_in
    bias_one = 1.0 - 0.9**10
    bias_two = 1.0 - 0.95**10
    update = first_out / bias_one / (jnp.sqrt(second_out / bias_two) + 1e-08)
    param_out = param_in - 0.25 * (update + 0.1 * param_in)
    return (param_out, first_out, second_out)


def clip_from(square_sum):
    clip_limit = 0.5 * math.sqrt(INNER * D + KCONV * CONV)
    return jnp.minimum(1.0, clip_limit / (jnp.sqrt(square_sum) + 1e-06))


def body(grad_proj, grad_conv, param_proj, m_proj, v_proj, ema_proj, param_conv, m_conv, v_conv):
    replica_count = lax.axis_size("rep") * lax.axis_size("dp")
    conv_avg = lax.psum(grad_conv[0], ("rep", "dp")) / replica_count
    conv_square = jnp.sum(conv_avg * conv_avg)
    first_owner = lax.axis_index("dp") == 0
    owner_sum = lax.psum_scatter(grad_proj[0], "dp", scatter_dimension=1, tiled=True)
    proj_avg = lax.psum(owner_sum, "rep") / replica_count
    conv_share = jnp.where(first_owner, conv_square, jnp.float32(0.0))
    square_sum = lax.psum(jnp.sum(proj_avg * proj_avg) + conv_share, ("dp", "tensor"))
    clip_factor = clip_from(square_sum)
    new_param_proj, new_m_proj, new_v_proj = adamw_step(
        param_proj, m_proj, v_proj, clip_factor * proj_avg
    )
    new_param_conv, new_m_conv, new_v_conv = adamw_step(
        param_conv, m_conv, v_conv, clip_factor * conv_avg
    )
    ema_count = ema_proj.shape[0]
    full_block = lax.all_gather(
        new_param_proj.astype(jnp.bfloat16), "dp", axis=1, tiled=True
    ).astype(new_param_proj.dtype)
    weights_proj = full_block.astype(jnp.bfloat16)
    row_block = lax.dynamic_slice_in_dim(full_block, lax.axis_index("dp") * ema_count, ema_count, 0)
    new_ema_proj = 0.9 * ema_proj + 0.1 * row_block
    return (
        new_param_proj,
        new_m_proj,
        new_v_proj,
        new_ema_proj,
        weights_proj,
        new_param_conv,
        new_m_conv,
        new_v_conv,
    )


def solution(mesh):
    in_specs = (
        P(("rep", "dp"), "tensor", None),
        P(("rep", "dp"), None, "tensor"),
        P("tensor", "dp"),
        P("tensor", "dp"),
        P("tensor", "dp"),
        P(("tensor", "dp"), None),
        P(None, "tensor"),
        P(None, "tensor"),
        P(None, "tensor"),
    )
    out_specs = (
        P("tensor", "dp"),
        P("tensor", "dp"),
        P("tensor", "dp"),
        P(("tensor", "dp"), None),
        P("tensor", None),
        P(None, "tensor"),
        P(None, "tensor"),
        P(None, "tensor"),
    )
    return jax.shard_map(body, mesh=mesh, in_specs=in_specs, out_specs=out_specs, check_vma=False)
```

profile of v0, /device:TPU:1, one launch (start us, length us, event | category | flops | bytes accessed | tf_op | source)
XLA Modules:
  0.0 549.1 jit_solution(13845586338401462347)
XLA Ops:
  7.2 0.0 reduce-scatter.2.cloned.1.call-start
  7.2 3.1 copy.19
  10.3 0.0 copy-start.8
  10.3 0.0 copy-start.2
  10.3 0.0 copy-start.3
  10.3 0.0 copy-start.4
  10.3 0.0 reduce-scatter.2.cloned.1.call-update
  10.3 0.0 copy-start.1
  10.3 0.0 all-reduce.2.cloned.1.call-start
  10.4 66.1 %reduce-scatter.2.cloned.1.call-done = f32[384,96]{0,1:T(8,128)} async-done(((f32[384,1536]{0,1:T(8,128)}), f32[384,96]{0,1:T(8,128)}) %reduce-scatter.2.cloned.1.call-update) | async-done | bytes 147472 | tf_op jit(solution)/shard_map/reduce_scatter | solution.py:34
  76.5 0.0 all-reduce.2.cloned.1.call-update
  76.5 0.0 copy-start.5
  76.5 0.0 copy-start.6
  76.5 0.0 copy-start.7
  76.5 0.0 all-gather.2.cloned.1.call-start
  76.6 0.0 copy-done.8
  76.6 142.5 %psum.22 = f32[4,416]{1,0:T(4,128)S(1)} all-reduce(f32[4,416]{1,0:T(4,128)S(1)} %bitcast.3), channel_id=1, replica_groups=mesh['rep'=4,'dp'=16,'tensor'=8] {'rep','dp'}, use_global_device_ids=true, to_apply=%region_3.0 | all-reduce | flops 1664 | bytes 13312 | tf_op jit(solution)/shard_map/psum | solution.py:31
  219.1 0.6 multiply_reduce_fusion.1
  220.3 0.0 all-reduce.2.cloned.1.call-done
  220.4 1.6 multiply_reduce_fusion
  222.6 270.7 %psum.23 = f32[]{:T(128)} all-reduce(f32[]{:T(128)S(6)} %add.50), channel_id=1, replica_groups=mesh['rep'=4,'dp'=16,'tensor'=8] {'dp','tensor'}, use_global_device_ids=true, to_apply=%region_5.6 | all-reduce | flops 1 | bytes 8 | tf_op jit(solution)/shard_map/psum | solution.py:37
  494.0 0.0 copy-done.2
  494.0 0.0 copy-done.3
  494.0 0.0 copy-done.4
  494.0 1.8 fusion.3
  495.7 0.0 all-gather.2.cloned.1.call-update
  495.8 0.0 copy-done.1
  495.8 0.3 copy.20
  496.1 0.0 copy-done.5
  496.1 0.0 copy-done.6
  496.1 0.0 copy-done.7
  496.1 0.6 multiply_subtract_fusion.1
  496.7 42.1 %all-gather.2.cloned.1.call-done = bf16[384,1536]{0,1:T(8,128)(2,1)} async-done(((bf16[384,96]{0,1:T(8,128)(2,1)}), bf16[384,1536]{0,1:T(8,128)(2,1)}) %all-gather.2.cloned.1.call-update) | async-done | bytes 1179664 | tf_op jit(solution)/shard_map/all_gather | solution.py:46
  538.8 0.0 copy-start
  538.8 1.4 multiply_add_fusion
  540.3 0.9 copy.21
  541.2 0.0 copy-done
  541.2 1.4 copy.22
Async XLA Ops:
  7.2 69.3 %reduce-scatter.2.cloned.1.call-start = ((), (), s32[]{:S(2)}) async-start(), calls=%async_computation.1 | async-start | bytes 2506752 | tf_op jit(solution)/shard_map/reduce_scatter | solution.py:34
  10.3 66.3 %copy-start.8 = (f32[1,4,416]{2,1,0:T(4,128)S(1)}, f32[1,4,416]{2,1,0:T(4,128)}, u32[]{:S(2)}) copy-start(f32[1,4,416]{2,1,0:T(4,128)} %param.10) | copy-start | bytes 19972
  10.3 483.7 %copy-start.2 = (f32[384,96]{0,1:T(8,128)S(1)}, f32[384,96]{0,1:T(8,128)}, u32[]{:S(2)}) copy-start(f32[384,96]{0,1:T(8,128)} %param.11) | copy-start | bytes 442372
  10.3 483.7 %copy-start.3 = (f32[384,96]{0,1:T(8,128)S(1)}, f32[384,96]{0,1:T(8,128)}, u32[]{:S(2)}) copy-start(f32[384,96]{0,1:T(8,128)} %param.12) | copy-start | bytes 442372
  10.3 483.7 %copy-start.4 = (f32[384,96]{0,1:T(8,128)S(1)}, f32[384,96]{0,1:T(8,128)}, u32[]{:S(2)}) copy-start(f32[384,96]{0,1:T(8,128)} %param.13) | copy-start | bytes 442372
  10.3 485.4 %copy-start.1 = (f32[24,1536]{1,0:T(8,128)S(1)}, f32[24,1536]{1,0:T(8,128)}, u32[]{:S(2)}) copy-start(f32[24,1536]{1,0:T(8,128)} %param.14) | copy-start | bytes 442372
  10.3 210.0 %all-reduce.2.cloned.1.call-start = ((), (), s32[]{:S(2)}) async-start(), calls=%async_computation.2 | async-start | bytes 294912 | tf_op jit(solution)/shard_map/psum | solution.py:35
  76.5 419.6 %copy-start.5 = (f32[4,416]{1,0:T(4,128)S(1)}, f32[4,416]{1,0:T(4,128)}, u32[]{:S(2)}) copy-start(f32[4,416]{1,0:T(4,128)} %param.15) | copy-start | bytes 19972
  76.5 419.5 %copy-start.6 = (f32[4,416]{1,0:T(4,128)S(1)}, f32[4,416]{1,0:T(4,128)}, u32[]{:S(2)}) copy-start(f32[4,416]{1,0:T(4,128)} %param.16) | copy-start | bytes 19972
  76.5 419.5 %copy-start.7 = (f32[4,416]{1,0:T(4,128)S(1)}, f32[4,416]{1,0:T(4,128)}, u32[]{:S(2)}) copy-start(f32[4,416]{1,0:T(4,128)} %param.17) | copy-start | bytes 19972
  76.5 462.3 %all-gather.2.cloned.1.call-start = ((), (), s32[]{:S(2)}) async-start(), calls=%async_computation.3 | async-start | bytes 1253376 | tf_op jit(solution)/shard_map/all_gather | solution.py:46
  538.8 2.3 copy-start
Sparse Core Ops, SparseCore 0:
  10.8 65.6 reduce-scatter.1
  79.4 55.1 all-reduce.1
  495.9 42.8 all-gather.1
where the time goes:
time: 549 us
  blocking collectives  413 us (75%)
  waiting for transfers between devices  108 us (20%)
  between operations  15.9 us (3%)
  other arithmetic  5.98 us (1%)
  local copies, waits for them, and re-layouts  5.74 us (1%)
    psum x1, blocking collectives, body(): lax.psum(jnp.sum(proj_avg * proj_avg) + conv_share, ('dp', 'tensor'))  271 us
    psum x1, blocking collectives, body(): conv_avg = lax.psum(grad_conv[0], ('rep', 'dp')) / replica_count  142 us
    reduce_scatter x1, waiting for transfers between devices, body(): lax.psum_scatter(grad_proj[0], 'dp', scatter_dimension=1, tiled=True)  66.1 us
    all_gather x1, waiting for transfers between devices, body(): lax.all_gather(new_param_proj.astype(jnp.bfloat16), 'dp', axis=1, tiled=T...  42.1 us
  transfers between devices with their start and end apart: 3, of which 2 were waited for; matrix products, arithmetic and copies ran while one was open for 0% of the time, Pallas kernels for 0%

commit v1 on v0

v1 whole, which is shorter than its diff:
```python
import functools
import math

import jax
import jax.numpy as jnp
from jax import lax
from jax.experimental import pallas as pl
from jax.experimental.pallas import tpu as pltpu
from jax.sharding import PartitionSpec as P

D = 1536
INNER = 3072
CONV = 3328
KCONV = 4

F32 = jnp.float32
BF16 = jnp.bfloat16
MESH = pl.DeviceIdType.MESH

YS = 8
REPS = 4
TENS = 8
ROWS = INNER // TENS
BLK = D // (2 * YS)
HALF = BLK // 2
QUART = BLK // REPS
CCOL = CONV // TENS
EROW = ROWS // (2 * YS)
SCALE_UP = 2.0**15
SCALE_DOWN = 2.0**-15


def adamw_step(param_in, first_in, second_in, grad_in):
    first_out = 0.9 * first_in + 0.1 * grad_in
    second_out = 0.95 * second_in + 0.05 * grad_in * grad_in
    bias_one = 1.0 - 0.9**10
    bias_two = 1.0 - 0.95**10
    update = first_out / bias_one / (jnp.sqrt(second_out / bias_two) + 1e-08)
    param_out = param_in - 0.25 * (update + 0.1 * param_in)
    return (param_out, first_out, second_out)


def clip_from(square_sum):
    clip_limit = 0.5 * math.sqrt(INNER * D + KCONV * CONV)
    return jnp.minimum(1.0, clip_limit / (jnp.sqrt(square_sum) + 1e-06))


def encode(x):
    wide = x * SCALE_UP
    square = wide * wide
    return ((square * wide) * jnp.abs(wide)).astype(BF16)


def signed_root(x):
    return x * lax.rsqrt(jnp.maximum(jnp.abs(x), 1e-37))


def decode(code):
    return signed_root(signed_root(code.astype(F32))) * SCALE_DOWN


def fold(x):
    total = x[0:8, 0:128]
    for i in range(x.shape[0] // 8):
        for j in range(x.shape[1] // 128):
            if i or j:
                total = total + x[8 * i : 8 * i + 8, 128 * j : 128 * j + 128]
    return total


P0, M1, P1, M0 = 0, 4, 8, 11
STREAMS = ((P0, 1, 0, 4), (M1, -1, 1, 4), (P1, 1, 1, 3), (M0, -1, 0, 3))


def kernel(
    grad, conv, param, mom, vel, ema, cparam, cmom, cvel,
    o_param, o_mom, o_vel, o_ema, o_weights, o_cparam, o_cmom, o_cvel,
    g_in, gt, pair_out, pair_in, ring_out, ring_in, zq_out, zq_in, zg, wt,
    p_v, m_v, v_v, e_v, conv_y, conv_c, conv_z, cp_v, cm_v, cv_v, norm_r, norm_d, norm_t,
    load_sem, pair_s, pair_r, ring_s, ring_r, zq_s, zq_r, zg_s, zg_r,
    gather_s, gather_r, share_s, share_r, cy_s, cy_r, cc_s, cc_r, cz_s, cz_r,
    nr_s, nr_r, nd_s, nd_r, nt_s, nt_r,
):
    rep = lax.axis_index("rep")
    dp = lax.axis_index("dp")
    ten = lax.axis_index("tensor")
    y = dp // 2
    core = dp % 2
    partner = 2 * y + (1 - core)

    def y_at(off):
        return (y + (off + YS)) % YS

    def remote(src, dst, send, recv, **device):
        return pltpu.make_async_remote_copy(
            src_ref=src, dst_ref=dst, send_sem=send, recv_sem=recv,
            device_id=device, device_id_type=MESH,
        )

    base = (y // 2 + 2) % 4
    turn = 2 * (y % 2) - 1
    order = (base, (base + turn + 4) % 4, (base - turn + 4) % 4, (base + 2) % 4)
    loads = []
    for i, group in enumerate(order):
        cols = pl.ds(pl.multiple_of(group * 384, 128), 384)
        loads.append(pltpu.make_async_copy(grad.at[:, cols], g_in.at[:, cols], load_sem.at[i]))
        loads[-1].start()
    conv_load = pltpu.make_async_copy(conv, conv_y.at[y], load_sem.at[4])
    conv_load.start()
    late = []
    for i, (src, dst) in enumerate(
        ((param, p_v), (mom, m_v), (vel, v_v), (ema, e_v), (cparam, cp_v), (cmom, cm_v), (cvel, cv_v))
    ):
        late.append(pltpu.make_async_copy(src, dst, load_sem.at[5 + i]))
        late[-1].start()

    barrier = pltpu.get_barrier_semaphore()

    def greet(axis, me, count):
        def step(i, carry):
            pl.semaphore_signal(
                barrier, inc=1, device_id={axis: (me + i) % count}, device_id_type=MESH
            )
            return carry

        lax.fori_loop(1, count, step, 0)

    greet("dp", dp, 2 * YS)
    greet("rep", rep, REPS)
    greet("tensor", ten, TENS)

    def turn_group(i):
        loads[i].wait()
        group = order[i]

        def step(j, carry):
            at = pl.multiple_of(group * 384 + j * 128, 128)
            gt[pl.ds(at, 128), :] = g_in[:, pl.ds(at, 128)].T
            return carry

        lax.fori_loop(0, 3, step, 0)
        for k in range(2):
            own = 2 * group + k
            rows = pl.ds(pl.multiple_of((2 * own + (1 - core)) * BLK, BLK), BLK)
            pair_out[own] = encode(gt[rows, :])

    def pair_copy(own):
        return remote(
            pair_out.at[own], pair_in.at[own], pair_s.at[own], pair_r.at[own], dp=partner
        )

    def conv_y_copy(off):
        return remote(
            conv_y.at[y], conv_y.at[y], cy_s.at[off], cy_r.at[y], dp=2 * y_at(off) + core
        )

    turn_group(0)
    conv_load.wait()
    pl.semaphore_wait(barrier, (2 * YS - 1) + (REPS - 1) + (TENS - 1))
    for k in range(2):
        pair_copy(2 * order[0] + k).start()
    for off in range(1, YS):
        conv_y_copy(off).start()
    for i in range(1, 4):
        turn_group(i)
        for k in range(2):
            pair_copy(2 * order[i] + k).start()

    arrived = set()

    def local_sum(off, half):
        own = y_at(off)
        if off % YS not in arrived:
            arrived.add(off % YS)
            pair_copy(own).wait_recv()
        rows = pl.ds(pl.multiple_of((2 * own + core) * BLK + half * HALF, 16), HALF)
        return gt[rows, :] + decode(pair_in[own, half * HALF : half * HALF + HALF, :])

    def ring_copy(first, sign, k):
        return remote(
            ring_out.at[first + k], ring_in.at[first + k], ring_s.at[first + k],
            ring_r.at[first + k], dp=2 * y_at(sign) + core,
        )

    def conv_c_copy():
        return remote(conv_c.at[core], conv_c.at[core], cc_s, cc_r, dp=partner)

    def conv_z_copy(off):
        return remote(
            conv_z.at[rep], conv_z.at[rep], cz_s.at[off], cz_r.at[rep], rep=(rep + off) % REPS
        )

    for k in range(4):
        for first, sign, half, hops in STREAMS:
            if k < hops:
                total = local_sum(sign * (hops - k), half)
                if k:
                    ring_copy(first, sign, k - 1).wait_recv()
                    total = total + decode(ring_in[first + k - 1])
                ring_out[first + k] = encode(total)
                ring_copy(first, sign, k).start()
        if k == 0:
            for off in range(1, YS):
                src = y_at(off)
                remote(conv_y.at[src], conv_y.at[src], cy_s.at[off], cy_r.at[src], dp=partner).wait_recv()
            total = conv_y[0]
            for i in range(1, YS):
                total = total + conv_y[i]
            conv_c[core] = total
            conv_c_copy().start()
        if k == 1:
            conv_c_copy().wait_recv()
            conv_z[rep] = conv_c[0] + conv_c[1]
            for off in range(1, REPS):
                conv_z_copy(off).start()

    halves = []
    for half, (first, sign), (other, other_sign) in ((0, (P0, 1), (M0, -1)), (1, (M1, -1), (P1, 1))):
        total = local_sum(0, half)
        ring_copy(other, other_sign, 2).wait_recv()
        total = total + decode(ring_in[other + 2])
        ring_copy(first, sign, 3).wait_recv()
        total = total + decode(ring_in[first + 3])
        halves.append(total)

    part = (halves[0][0:QUART], halves[0][QUART:], halves[1][0:QUART], halves[1][QUART:])
    for q in range(REPS):
        zq_out[q] = encode(part[q])
        gt[q * QUART : (q + 1) * QUART, :] = part[q]

    def zq_copy(off):
        to = (rep + off) % REPS
        return remote(zq_out.at[to], zq_in.at[rep], zq_s.at[off], zq_r.at[rep], rep=to)

    for off in range(1, REPS):
        zq_copy(off).start()

    for off in range(1, REPS):
        src = (rep + off) % REPS
        remote(conv_z.at[src], conv_z.at[src], cz_s.at[off], cz_r.at[src], dp=partner).wait_recv()
    count = float(REPS * 2 * YS)
    conv_avg = (((conv_z[0] + conv_z[1]) + conv_z[2]) + conv_z[3]) * (1.0 / count)
    conv_square = jnp.sum(conv_avg * conv_avg) * (1.0 / count)

    avg = gt[pl.ds(pl.multiple_of(rep * QUART, 8), QUART), :]
    for off in range(1, REPS):
        src = (rep + off) % REPS
        remote(zq_out.at[src], zq_in.at[src], zq_s.at[off], zq_r.at[src], dp=partner).wait_recv()
        avg = avg + decode(zq_in[src])
    avg = avg * (1.0 / count)
    zg[rep] = encode(avg)

    def zg_copy(off):
        return remote(zg.at[rep], zg.at[rep], zg_s.at[off], zg_r.at[rep], rep=(rep + off) % REPS)

    def spread(buf, send, recv, axis, me, size):
        def start(i, carry):
            to = (me + i) % size
            remote(buf.at[me], buf.at[me], send.at[i], recv.at[me], **{axis: to}).start()
            return carry

        lax.fori_loop(1, size, start, 0)

    def collect(buf, send, recv, axis, me, size):
        def wait(i, carry):
            src = (me + i) % size
            remote(buf.at[src], buf.at[src], send.at[i], recv.at[src], **{axis: src}).wait_recv()
            return carry

        lax.fori_loop(1, size, wait, 0)
        total = buf[0]
        for i in range(1, size):
            total = total + buf[i]
        return total

    def drain(buf, send, recv, axis, me, size):
        def wait(i, carry):
            to = (me + i) % size
            remote(buf.at[me], buf.at[me], send.at[i], recv.at[me], **{axis: to}).wait_send()
            return carry

        lax.fori_loop(1, size, wait, 0)

    norm_r[rep] = fold(avg * avg)
    spread(norm_r, nr_s, nr_r, "rep", rep, REPS)
    for off in range(1, REPS):
        zg_copy(off).start()
    norm_d[dp] = collect(norm_r, nr_s, nr_r, "rep", rep, REPS)
    spread(norm_d, nd_s, nd_r, "dp", dp, 2 * YS)
    norm_t[ten] = collect(norm_d, nd_s, nd_r, "dp", dp, 2 * YS) + conv_square * (float(REPS * 2 * YS) / 1024.0)
    spread(norm_t, nt_s, nt_r, "tensor", ten, TENS)

    for off in range(1, REPS):
        src = (rep + off) % REPS
        remote(zg.at[src], zg.at[src], zg_s.at[off], zg_r.at[src], dp=partner).wait_recv()
    for q in range(REPS):
        gt[q * QUART : (q + 1) * QUART, :] = decode(zg[q])
    for copy in late:
        copy.wait()

    square_sum = jnp.sum(collect(norm_t, nt_s, nt_r, "tensor", ten, TENS), keepdims=True)
    clip = clip_from(square_sum)

    new_param, new_mom, new_vel = adamw_step(p_v[...], m_v[...], v_v[...], clip * gt[0:BLK, :])
    mine = pl.multiple_of(dp * BLK, BLK)
    wt[pl.ds(mine, BLK), :] = new_param.astype(BF16)

    def gather_copy(first, sign, half, k):
        own = y_at(-sign * k)
        rows = pl.ds(pl.multiple_of((2 * own + core) * BLK + half * HALF, 16), HALF)
        return remote(
            wt.at[rows, :], wt.at[rows, :], gather_s.at[first + k], gather_r.at[first + k],
            dp=2 * y_at(sign) + core,
        )

    def share_copy(off, half, whose):
        own = y_at(off)
        at = (2 * own + whose) * BLK + half * HALF
        rows = pl.ds(pl.multiple_of(at, 16), HALF)
        slot = (off % YS) * 2 + half
        return remote(wt.at[rows, :], wt.at[rows, :], share_s.at[slot], share_r.at[slot], dp=partner)

    for first, sign, half, hops in STREAMS:
        gather_copy(first, sign, half, 0).start()
    for half in range(2):
        share_copy(0, half, core).start()

    o_param[...] = new_param
    o_mom[...] = new_mom
    o_vel[...] = new_vel
    new_cparam, new_cmom, new_cvel = adamw_step(cp_v[...], cm_v[...], cv_v[...], clip * conv_avg)
    o_cparam[...] = new_cparam
    o_cmom[...] = new_cmom
    o_cvel[...] = new_cvel

    for k in range(1, 5):
        for first, sign, half, hops in STREAMS:
            if k <= hops:
                gather_copy(first, sign, half, k - 1).wait_recv()
                if k < hops:
                    gather_copy(first, sign, half, k).start()
                share_copy(-sign * k, half, core).start()

    for off in range(YS):
        for half in range(2):
            share_copy(off, half, 1 - core).wait_recv()

    def back(j, carry):
        at = pl.multiple_of(j * 128, 128)
        o_weights[:, pl.ds(at, 128)] = wt[pl.ds(at, 128), :].astype(F32).T.astype(BF16)
        return carry

    lax.fori_loop(0, D // 128, back, 0)
    near = o_weights[pl.ds(pl.multiple_of(y * 2 * EROW, 16), 2 * EROW), :].astype(F32)
    row_block = jnp.where(core == 0, near[0:EROW], near[EROW:])
    o_ema[...] = 0.9 * e_v[...] + 0.1 * row_block

    for off in range(YS):
        pair_copy(y_at(off)).wait_send()
    for first, sign, half, hops in STREAMS:
        for k in range(hops):
            ring_copy(first, sign, k).wait_send()
            gather_copy(first, sign, half, k).wait_send()
    for off in range(YS):
        for half in range(2):
            share_copy(off, half, core).wait_send()
    for off in range(1, YS):
        conv_y_copy(off).wait_send()
    conv_c_copy().wait_send()
    for off in range(1, REPS):
        conv_z_copy(off).wait_send()
        zq_copy(off).wait_send()
        zg_copy(off).wait_send()
    drain(norm_r, nr_s, nr_r, "rep", rep, REPS)
    drain(norm_d, nd_s, nd_r, "dp", dp, 2 * YS)
    drain(norm_t, nt_s, nt_r, "tensor", ten, TENS)


def body(grad_proj, grad_conv, param_proj, m_proj, v_proj, ema_proj, param_conv, m_conv, v_conv):
    small = jax.ShapeDtypeStruct((KCONV, CCOL), F32)
    block = jax.ShapeDtypeStruct((BLK, ROWS), F32)
    dma = pltpu.SemaphoreType.DMA
    outs = pl.pallas_call(
        kernel,
        out_shape=(
            block, block, block,
            jax.ShapeDtypeStruct((EROW, D), F32),
            jax.ShapeDtypeStruct((ROWS, D), BF16),
            small, small, small,
        ),
        in_specs=[pl.BlockSpec(memory_space=pltpu.HBM)] * 9,
        out_specs=[pl.BlockSpec(memory_space=pltpu.VMEM)] * 8,
        scratch_shapes=[
            pltpu.VMEM((ROWS, D), F32),
            pltpu.VMEM((D, ROWS), F32),
            pltpu.VMEM((YS, BLK, ROWS), BF16),
            pltpu.VMEM((YS, BLK, ROWS), BF16),
            pltpu.VMEM((14, HALF, ROWS), BF16),
            pltpu.VMEM((14, HALF, ROWS), BF16),
            pltpu.VMEM((REPS, QUART, ROWS), BF16),
            pltpu.VMEM((REPS, QUART, ROWS), BF16),
            pltpu.VMEM((REPS, QUART, ROWS), BF16),
            pltpu.VMEM((D, ROWS), BF16),
            pltpu.VMEM((BLK, ROWS), F32),
            pltpu.VMEM((BLK, ROWS), F32),
            pltpu.VMEM((BLK, ROWS), F32),
            pltpu.VMEM((EROW, D), F32),
            pltpu.VMEM((YS, KCONV, CCOL), F32),
            pltpu.VMEM((2, KCONV, CCOL), F32),
            pltpu.VMEM((REPS, KCONV, CCOL), F32),
            pltpu.VMEM((KCONV, CCOL), F32),
            pltpu.VMEM((KCONV, CCOL), F32),
            pltpu.VMEM((KCONV, CCOL), F32),
            pltpu.VMEM((REPS, 8, 128), F32),
            pltpu.VMEM((2 * YS, 8, 128), F32),
            pltpu.VMEM((TENS, 8, 128), F32),
            dma((12,)),
            dma((YS,)), dma((YS,)),
            dma((14,)), dma((14,)),
            dma((REPS,)), dma((REPS,)),
            dma((REPS,)), dma((REPS,)),
            dma((14,)), dma((14,)),
            dma((2 * YS,)), dma((2 * YS,)),
            dma((YS,)), dma((YS,)),
            dma, dma,
            dma((REPS,)), dma((REPS,)),
            dma((REPS,)), dma((REPS,)),
            dma((2 * YS,)), dma((2 * YS,)),
            dma((TENS,)), dma((TENS,)),
        ],
        compiler_params=pltpu.CompilerParams(
            collective_id=0, has_side_effects=True, vmem_limit_bytes=48 << 20
        ),
        name="adamw_step",
    )(
        grad_proj[0], grad_conv[0], param_proj.T, m_proj.T, v_proj.T, ema_proj,
        param_conv, m_conv, v_conv,
    )
    new_param, new_m, new_v, new_ema, weights, new_cparam, new_cm, new_cv = outs
    return (new_param.T, new_m.T, new_v.T, new_ema, weights, new_cparam, new_cm, new_cv)


def solution(mesh):
    in_specs = (
        P(("rep", "dp"), "tensor", None),
        P(("rep", "dp"), None, "tensor"),
        P("tensor", "dp"),
        P("tensor", "dp"),
        P("tensor", "dp"),
        P(("tensor", "dp"), None),
        P(None, "tensor"),
        P(None, "tensor"),
        P(None, "tensor"),
    )
    out_specs = (
        P("tensor", "dp"),
        P("tensor", "dp"),
        P("tensor", "dp"),
        P(("tensor", "dp"), None),
        P("tensor", None),
        P(None, "tensor"),
        P(None, "tensor"),
        P(None, "tensor"),
    )
    return jax.shard_map(body, mesh=mesh, in_specs=in_specs, out_specs=out_specs, check_vma=False)
```

time: 549 us -> 82.8 us (0.15)
  blocking collectives: 413 us -> 0 us
  waiting for transfers between devices: 108 us -> 0 us
  Pallas kernels: 0 us -> 68.2 us
  between operations: 15.9 us -> 0.66 us
  local copies, waits for them, and re-layouts: 5.74 us -> 13.5 us
  other arithmetic: 5.98 us -> 0 us
    psum x2 -> x0, blocking collectives: 413 us -> none  [the longest x1 271 us: body(): lax.psum(jnp.sum(proj_avg * proj_avg) + conv_share, ('dp', 'tensor'))]
    pallas_call x0 -> x1, Pallas kernels: none -> 68.2 us  [body(): pl.pallas_call(kernel, out_shape=(block, block, block, jax.ShapeDtypeStru...]
    reduce_scatter x1 -> x0, waiting for transfers between devices: 66.1 us -> none  [body(): lax.psum_scatter(grad_proj[0], 'dp', scatter_dimension=1, tiled=True)]
    all_gather x1 -> x0, waiting for transfers between devices: 42.1 us -> none  [body(): lax.all_gather(new_param_proj.astype(jnp.bfloat16), 'dp', axis=1, tiled=T...]
    unnamed x22 -> x26, local copies, waits for them, and re-layouts: 5.74 us -> 13.5 us
  transfers between devices with their start and end apart: 3 -> 0, of which waited for: 2 -> 0; matrix products, arithmetic and copies ran while one was open for 0% -> 0% of each run, Pallas kernels for 0% -> 0%
where the time goes in v1:
time: 82.8 us; the launch traced here: 82.4 us
  Pallas kernels  68.2 us (82%)
  local copies, waits for them, and re-layouts  13.5 us (16%)
    pallas_call x1, Pallas kernels, body(): pl.pallas_call(kernel, out_shape=(block, block, block, jax.ShapeDtypeStru...  68.2 us
    unnamed x26, local copies, waits for them, and re-layouts  13.5 us

profile of v1, /device:TPU:1, one launch (start us, length us, event | category | flops | bytes accessed | tf_op | source)
XLA Modules:
  0.0 82.4 jit_solution(10643907257479502225)
XLA Ops:
  0.6 0.0 copy-start
  0.6 1.7 %copy-done = f32[1,384,1536]{2,1,0:T(8,128)S(1)} copy-done((f32[1,384,1536]{2,1,0:T(8,128)S(1)}, f32[1,384,1536]{2,1,0:T(8,128)}, u32[]{:S(2)}) %copy-start) | copy-done | bytes 2359320
  2.3 0.0 copy-start.1
  2.3 0.9 %copy-done.1 = f32[384,96]{0,1:T(8,128)S(1)} copy-done((f32[384,96]{0,1:T(8,128)S(1)}, f32[384,96]{0,1:T(8,128)}, u32[]{:S(2)}) %copy-start.1) | copy-done | bytes 147480
  3.2 0.0 copy-start.2
  3.2 0.9 %copy-done.2 = f32[384,96]{0,1:T(8,128)S(1)} copy-done((f32[384,96]{0,1:T(8,128)S(1)}, f32[384,96]{0,1:T(8,128)}, u32[]{:S(2)}) %copy-start.2) | copy-done | bytes 147480
  4.1 0.0 copy-start.3
  4.1 0.9 %copy-done.3 = f32[384,96]{0,1:T(8,128)S(1)} copy-done((f32[384,96]{0,1:T(8,128)S(1)}, f32[384,96]{0,1:T(8,128)}, u32[]{:S(2)}) %copy-start.3) | copy-done | bytes 147480
  5.0 0.0 copy-start.4
  5.0 0.9 %copy-done.4 = f32[24,1536]{1,0:T(8,128)S(1)} copy-done((f32[24,1536]{1,0:T(8,128)S(1)}, f32[24,1536]{1,0:T(8,128)}, u32[]{:S(2)}) %copy-start.4) | copy-done | bytes 147480
  5.9 0.0 copy-start.5
  5.9 0.7 copy-done.5
  6.6 0.0 copy-start.6
  6.6 0.7 copy-done.6
  7.3 0.0 copy-start.7
  7.3 0.7 copy-done.7
  8.0 0.0 copy-start.8
  8.0 0.7 copy-done.8
  8.7 68.2 %adamw_step.1 = (f32[96,384]{1,0:T(8,128)S(1)}, f32[96,384]{1,0:T(8,128)S(1)}, f32[96,384]{1,0:T(8,128)S(1)}, f32[24,1536]{1,0:T(8,128)S(1)}, bf16[384,1536]{1,0...) custom-call(f32[384,1536]{1,0:T(8,128)S(1)} %bitcast.8, ...), custom_call_target="tpu_custom_call" | custom-call | tf_op jit(solution)/shard_map/adamw_step/pallas_call | solution.py:383
  76.9 0.7 copy.25
  77.6 0.7 copy.26
  78.2 0.7 copy.27
  78.9 0.7 copy.28
  79.5 1.0 %copy.29 = bf16[384,1536]{1,0:T(8,128)(2,1)} copy(bf16[384,1536]{1,0:T(8,128)(2,1)S(1)} %get-tuple-element.36) | data formatting | bytes 2359296
  80.6 0.6 copy.30
  81.2 0.6 copy.31
  81.8 0.6 copy.32
Async XLA Ops:
  0.6 1.7 %copy-start = (f32[1,384,1536]{2,1,0:T(8,128)S(1)}, f32[1,384,1536]{2,1,0:T(8,128)}, u32[]{:S(2)}) copy-start(f32[1,384,1536]{2,1,0:T(8,128)} %param.9) | copy-start | bytes 7077892
  2.3 0.9 %copy-start.1 = (f32[384,96]{0,1:T(8,128)S(1)}, f32[384,96]{0,1:T(8,128)}, u32[]{:S(2)}) copy-start(f32[384,96]{0,1:T(8,128)} %param.11) | copy-start | bytes 442372
  3.2 0.9 %copy-start.2 = (f32[384,96]{0,1:T(8,128)S(1)}, f32[384,96]{0,1:T(8,128)}, u32[]{:S(2)}) copy-start(f32[384,96]{0,1:T(8,128)} %param.12) | copy-start | bytes 442372
  4.1 0.9 %copy-start.3 = (f32[384,96]{0,1:T(8,128)S(1)}, f32[384,96]{0,1:T(8,128)}, u32[]{:S(2)}) copy-start(f32[384,96]{0,1:T(8,128)} %param.13) | copy-start | bytes 442372
  5.0 0.9 %copy-start.4 = (f32[24,1536]{1,0:T(8,128)S(1)}, f32[24,1536]{1,0:T(8,128)}, u32[]{:S(2)}) copy-start(f32[24,1536]{1,0:T(8,128)} %ema.1) | copy-start | bytes 442372
  5.9 0.7 copy-start.5
  6.6 0.7 copy-start.6
  7.3 0.7 copy-start.7
  8.0 0.7 copy-start.8

commit v2 on v1

v2 whole, which is shorter than its diff:
```python
import functools
import math

import jax
import jax.numpy as jnp
from jax import lax
from jax.experimental import pallas as pl
from jax.experimental.pallas import tpu as pltpu
from jax.sharding import PartitionSpec as P

D = 1536
INNER = 3072
CONV = 3328
KCONV = 4

F32 = jnp.float32
BF16 = jnp.bfloat16
MESH = pl.DeviceIdType.MESH

YS = 8
REPS = 4
TENS = 8
ROWS = INNER // TENS
BLK = D // (2 * YS)
HALF = BLK // 2
CCOL = CONV // TENS
EROW = ROWS // (2 * YS)
SCALE_UP = 2.0**15
SCALE_DOWN = 2.0**-15


def adamw_step(param_in, first_in, second_in, grad_in):
    first_out = 0.9 * first_in + 0.1 * grad_in
    second_out = 0.95 * second_in + 0.05 * grad_in * grad_in
    bias_one = 1.0 - 0.9**10
    bias_two = 1.0 - 0.95**10
    update = first_out / bias_one / (jnp.sqrt(second_out / bias_two) + 1e-08)
    param_out = param_in - 0.25 * (update + 0.1 * param_in)
    return (param_out, first_out, second_out)


def clip_from(square_sum):
    clip_limit = 0.5 * math.sqrt(INNER * D + KCONV * CONV)
    return jnp.minimum(1.0, clip_limit / (jnp.sqrt(square_sum) + 1e-06))


def encode(x):
    wide = x * SCALE_UP
    square = wide * wide
    return ((square * wide) * jnp.abs(wide)).astype(BF16)


def signed_root(x):
    return x * lax.rsqrt(jnp.maximum(jnp.abs(x), 1e-37))


def decode(code):
    return signed_root(signed_root(code.astype(F32))) * SCALE_DOWN


def fold(x):
    total = x[0:8, 0:128]
    for i in range(x.shape[0] // 8):
        for j in range(x.shape[1] // 128):
            if i or j:
                total = total + x[8 * i : 8 * i + 8, 128 * j : 128 * j + 128]
    return total


WAYS = ((1, 0), (-1, 1))


def kernel(
    grad, conv, param, mom, vel, ema, cparam, cmom, cvel,
    o_param, o_mom, o_vel, o_ema, o_weights, o_cparam, o_cmom, o_cvel,
    g_in, gt, pair_out, pair_in, far_out, far_in, mid_out, mid_in, rel_out, rel_in, near_out, near_in,
    zx, wt, p_v, m_v, v_v, e_v, conv_y, conv_c, conv_z, cp_v, cm_v, cv_v, norm_d, norm_t,
    load_sem, pair_s, pair_r, far_s, far_r, mid_s, mid_r, rel_s, rel_r, near_s, near_r, zx_s, zx_r,
    own_s, own_r, fwd_s, fwd_r, share_s, share_r, cy_s, cy_r, cc_s, cc_r, cz_s, cz_r,
    nd_s, nd_r, nt_s, nt_r,
):
    rep = lax.axis_index("rep")
    dp = lax.axis_index("dp")
    ten = lax.axis_index("tensor")
    y = dp // 2
    core = dp % 2
    partner = 2 * y + (1 - core)

    def y_at(off):
        return (y + (off + YS)) % YS

    def remote(src, dst, send, recv, **device):
        return pltpu.make_async_remote_copy(
            src_ref=src, dst_ref=dst, send_sem=send, recv_sem=recv,
            device_id=device, device_id_type=MESH,
        )

    base = (y // 2 + 2) % 4
    turn = 2 * (y % 2) - 1
    order = (base, (base + turn + 4) % 4, (base - turn + 4) % 4, (base + 2) % 4)
    loads = []
    for i, group in enumerate(order):
        cols = pl.ds(pl.multiple_of(group * 384, 128), 384)
        loads.append(pltpu.make_async_copy(grad.at[:, cols], g_in.at[:, cols], load_sem.at[i]))
        loads[-1].start()
    conv_load = pltpu.make_async_copy(conv, conv_y.at[y], load_sem.at[4])
    conv_load.start()
    late = []
    for i, (src, dst) in enumerate(
        ((param, p_v), (mom, m_v), (vel, v_v), (ema, e_v), (cparam, cp_v), (cmom, cm_v), (cvel, cv_v))
    ):
        late.append(pltpu.make_async_copy(src, dst, load_sem.at[5 + i]))
        late[-1].start()

    barrier = pltpu.get_barrier_semaphore()

    def greet(axis, me, count):
        def step(i, carry):
            pl.semaphore_signal(
                barrier, inc=1, device_id={axis: (me + i) % count}, device_id_type=MESH
            )
            return carry

        lax.fori_loop(1, count, step, 0)

    greet("dp", dp, 2 * YS)
    greet("rep", rep, REPS)
    greet("tensor", ten, TENS)

    def turn_group(i):
        loads[i].wait()
        group = order[i]

        def step(j, carry):
            at = pl.multiple_of(group * 384 + j * 128, 128)
            gt[pl.ds(at, 128), :] = g_in[:, pl.ds(at, 128)].T
            return carry

        lax.fori_loop(0, 3, step, 0)
        for k in range(2):
            own = 2 * group + k
            rows = pl.ds(pl.multiple_of((2 * own + (1 - core)) * BLK, BLK), BLK)
            pair_out[own] = encode(gt[rows, :])

    def pair_copy(own):
        return remote(
            pair_out.at[own], pair_in.at[own], pair_s.at[own], pair_r.at[own], dp=partner
        )

    def conv_y_copy(off):
        return remote(
            conv_y.at[y], conv_y.at[y], cy_s.at[off], cy_r.at[y], dp=2 * y_at(off) + core
        )

    turn_group(0)
    conv_load.wait()
    pl.semaphore_wait(barrier, (2 * YS - 1) + (REPS - 1) + (TENS - 1))
    for k in range(2):
        pair_copy(2 * order[0] + k).start()
    for off in range(1, YS):
        conv_y_copy(off).start()
    for i in range(1, 4):
        turn_group(i)
        for k in range(2):
            pair_copy(2 * order[i] + k).start()

    arrived = set()

    def local_sum(off, half=None):
        own = y_at(off)
        if off % YS not in arrived:
            arrived.add(off % YS)
            pair_copy(own).wait_recv()
        lo, n = (0, BLK) if half is None else (half * HALF, HALF)
        rows = pl.ds(pl.multiple_of((2 * own + core) * BLK + lo, 16), n)
        return gt[rows, :] + decode(pair_in[own, lo : lo + n, :])

    def y_copy(out, into, send, recv, i, hops):
        return remote(out.at[i], into.at[i], send.at[i], recv.at[i], dp=2 * y_at(hops) + core)

    def far_copy(i):
        return y_copy(far_out, far_in, far_s, far_r, i, 2 * WAYS[i][0])

    def mid_copy(i):
        return y_copy(mid_out, mid_in, mid_s, mid_r, i, WAYS[i][0])

    def rel_copy(i, half):
        return y_copy(rel_out, rel_in, rel_s, rel_r, 2 * i + half, 2 * WAYS[i][0])

    def near_copy(i):
        return y_copy(near_out, near_in, near_s, near_r, i, WAYS[i][0])

    def conv_c_copy():
        return remote(conv_c.at[core], conv_c.at[core], cc_s, cc_r, dp=partner)

    def conv_z_copy(off):
        return remote(
            conv_z.at[rep], conv_z.at[rep], cz_s.at[off], cz_r.at[rep], rep=(rep + off) % REPS
        )

    for i, (sign, half) in enumerate(WAYS):
        far_out[i] = encode(local_sum(4 * sign, half))
        far_copy(i).start()
    for i, (sign, _) in enumerate(WAYS):
        mid_out[i] = encode(local_sum(3 * sign))
        mid_copy(i).start()
    for i, (sign, _) in enumerate(WAYS):
        near_out[i] = encode(local_sum(sign))
        near_copy(i).start()

    for off in range(1, YS):
        src = y_at(off)
        remote(conv_y.at[src], conv_y.at[src], cy_s.at[off], cy_r.at[src], dp=partner).wait_recv()
    total = conv_y[0]
    for i in range(1, YS):
        total = total + conv_y[i]
    conv_c[core] = total
    conv_c_copy().start()
    for i, (sign, half) in enumerate(WAYS):
        mid_copy(i).wait_recv()
        far_copy(i).wait_recv()
        for h in (half, 1 - half):
            total = local_sum(2 * sign, h) + decode(mid_in[i, h * HALF : (h + 1) * HALF, :])
            if h == half:
                total = total + decode(far_in[i])
            rel_out[2 * i + h] = encode(total)
            rel_copy(i, h).start()
    conv_c_copy().wait_recv()
    conv_z[rep] = conv_c[0] + conv_c[1]
    for off in range(1, REPS):
        conv_z_copy(off).start()

    mine_sum = [local_sum(0, h) for h in range(2)]
    for i in range(2):
        near_copy(i).wait_recv()
        for h in range(2):
            mine_sum[h] = mine_sum[h] + decode(near_in[i, h * HALF : (h + 1) * HALF, :])

    def zx_copy(off, h):
        return remote(
            zx.at[2 * rep + h], zx.at[2 * rep + h], zx_s.at[2 * off + h], zx_r.at[2 * rep + h],
            rep=(rep + off) % REPS,
        )

    for h in range(2):
        for i in range(2):
            rel_copy(i, h).wait_recv()
            mine_sum[h] = mine_sum[h] + decode(rel_in[2 * i + h])
        zx[2 * rep + h] = encode(mine_sum[h])
        for off in (2, 1, 3):
            zx_copy(off, h).start()

    for off in range(1, REPS):
        src = (rep + off) % REPS
        remote(conv_z.at[src], conv_z.at[src], cz_s.at[off], cz_r.at[src], dp=partner).wait_recv()
    count = float(REPS * 2 * YS)
    conv_avg = (((conv_z[0] + conv_z[1]) + conv_z[2]) + conv_z[3]) * (1.0 / count)
    conv_square = jnp.sum(conv_avg * conv_avg)

    avg = []
    for h in range(2):
        for off in range(1, REPS):
            src = 2 * ((rep + off) % REPS) + h
            remote(zx.at[src], zx.at[src], zx_s.at[2 * off + h], zx_r.at[src], dp=partner).wait_recv()
        total = decode(zx[h])
        for r in range(1, REPS):
            total = total + decode(zx[2 * r + h])
        avg.append(total * (1.0 / count))

    def row_copy(buf, send, recv, axis, me, i, size):
        to = (me + i) % size
        at = buf.at[me, pl.ds(0, 1), :]
        return remote(at, at, send.at[i], recv.at[me], **{axis: to})

    def spread(buf, send, recv, axis, me, size):
        def start(i, carry):
            row_copy(buf, send, recv, axis, me, i, size).start()
            return carry

        lax.fori_loop(1, size, start, 0)

    def collect(buf, send, recv, axis, me, size):
        def wait(i, carry):
            src = (me + i) % size
            at = buf.at[src, pl.ds(0, 1), :]
            remote(at, at, send.at[i], recv.at[src], **{axis: src}).wait_recv()
            return carry

        lax.fori_loop(1, size, wait, 0)
        total = buf[0, 0:1, :]
        for i in range(1, size):
            total = total + buf[i, 0:1, :]
        return total

    def drain(buf, send, recv, axis, me, size):
        def wait(i, carry):
            row_copy(buf, send, recv, axis, me, i, size).wait_send()
            return carry

        lax.fori_loop(1, size, wait, 0)

    square = fold(avg[0] * avg[0]) + fold(avg[1] * avg[1])
    norm_d[dp, 0:1, :] = jnp.sum(square, axis=0, keepdims=True)
    spread(norm_d, nd_s, nd_r, "dp", dp, 2 * YS)
    for h in range(2):
        gt[h * HALF : (h + 1) * HALF, :] = avg[h]
    for copy in late:
        copy.wait()
    norm_t[ten, 0:1, :] = collect(norm_d, nd_s, nd_r, "dp", dp, 2 * YS) + conv_square * (1.0 / 128.0)
    spread(norm_t, nt_s, nt_r, "tensor", ten, TENS)

    square_sum = jnp.sum(collect(norm_t, nt_s, nt_r, "tensor", ten, TENS), keepdims=True)
    clip = clip_from(square_sum)

    new_param, new_mom, new_vel = adamw_step(p_v[...], m_v[...], v_v[...], clip * gt[0:BLK, :])
    mine = pl.multiple_of(dp * BLK, BLK)
    wt[pl.ds(mine, BLK), :] = new_param.astype(BF16)

    def rows_of(off, whose, half=None):
        lo, n = (0, BLK) if half is None else (half * HALF, HALF)
        return pl.ds(pl.multiple_of((2 * y_at(off) + whose) * BLK + lo, 16), n)

    def gather_copy(send, recv, slot, off, half, hops):
        rows = rows_of(off, core, half)
        return remote(
            wt.at[rows, :], wt.at[rows, :], send.at[slot], recv.at[slot], dp=2 * y_at(hops) + core
        )

    def own2_copy(i, half):
        return gather_copy(own_s, own_r, 2 * i + half, 0, half, 2 * WAYS[i][0])

    def own1_copy(i):
        return gather_copy(own_s, own_r, 4 + i, 0, None, WAYS[i][0])

    def fwd1_copy(i, half):
        return gather_copy(fwd_s, fwd_r, 2 * i + half, -2 * WAYS[i][0], half, WAYS[i][0])

    def fwd2_copy(i):
        sign, half = WAYS[i]
        return gather_copy(fwd_s, fwd_r, 4 + i, -2 * sign, half, 2 * sign)

    def share_copy(off, half, whose):
        rows = rows_of(off, whose, half)
        slot = 2 * y_at(off) + (half or 0)
        return remote(wt.at[rows, :], wt.at[rows, :], share_s.at[slot], share_r.at[slot], dp=partner)

    for k in range(2):
        for i, (sign, half) in enumerate(WAYS):
            own2_copy(i, half if k == 0 else 1 - half).start()
    for i in range(2):
        own1_copy(i).start()
    share_copy(0, None, core).start()

    o_param[...] = new_param
    o_mom[...] = new_mom
    o_vel[...] = new_vel
    new_cparam, new_cmom, new_cvel = adamw_step(cp_v[...], cm_v[...], cv_v[...], clip * conv_avg)
    o_cparam[...] = new_cparam
    o_cmom[...] = new_cmom
    o_cvel[...] = new_cvel

    for k in range(2):
        for i, (sign, half) in enumerate(WAYS):
            h = half if k == 0 else 1 - half
            own2_copy(i, h).wait_recv()
            if k == 0:
                fwd2_copy(i).start()
            fwd1_copy(i, h).start()
            share_copy(-2 * sign, h, core).start()
    for i, (sign, _) in enumerate(WAYS):
        own1_copy(i).wait_recv()
        share_copy(-sign, None, core).start()

    def back(first):
        def step(j, carry):
            at = pl.multiple_of(first * 192 + j * 128, 128)
            o_weights[:, pl.ds(at, 128)] = wt[pl.ds(at, 128), :].astype(F32).T.astype(BF16)
            return carry

        lax.fori_loop(0, 3, step, 0)

    share_copy(0, None, 1 - core).wait_recv()
    for sign, _ in WAYS:
        share_copy(-sign, None, 1 - core).wait_recv()
        for h in range(2):
            share_copy(-2 * sign, h, 1 - core).wait_recv()
    pair = y // 2
    back(2 * pair)
    back(2 * ((pair + turn + 4) % 4))
    for i, (sign, half) in enumerate(WAYS):
        fwd2_copy(i).wait_recv()
        share_copy(-4 * sign, half, core).start()
    for k in range(2):
        for i, (sign, half) in enumerate(WAYS):
            h = half if k == 0 else 1 - half
            fwd1_copy(i, h).wait_recv()
            share_copy(-3 * sign, h, core).start()
    for off in (4, 3, -3):
        for h in range(2):
            share_copy(off, h, 1 - core).wait_recv()
    back(2 * ((pair - turn + 4) % 4))
    back(2 * ((pair + 2) % 4))
    near = o_weights[pl.ds(pl.multiple_of(y * 2 * EROW, 16), 2 * EROW), :].astype(F32)
    row_block = jnp.where(core == 0, near[0:EROW], near[EROW:])
    o_ema[...] = 0.9 * e_v[...] + 0.1 * row_block

    for off in range(YS):
        pair_copy(y_at(off)).wait_send()
    for i, (sign, half) in enumerate(WAYS):
        far_copy(i).wait_send()
        mid_copy(i).wait_send()
        near_copy(i).wait_send()
        own1_copy(i).wait_send()
        fwd2_copy(i).wait_send()
        share_copy(-sign, None, core).wait_send()
        share_copy(-4 * sign, half, core).wait_send()
        for h in range(2):
            rel_copy(i, h).wait_send()
            own2_copy(i, h).wait_send()
            fwd1_copy(i, h).wait_send()
            share_copy(-2 * sign, h, core).wait_send()
            share_copy(-3 * sign, h, core).wait_send()
    share_copy(0, None, core).wait_send()
    for off in range(1, YS):
        conv_y_copy(off).wait_send()
    conv_c_copy().wait_send()
    for off in range(1, REPS):
        conv_z_copy(off).wait_send()
        for h in range(2):
            zx_copy(off, h).wait_send()
    drain(norm_d, nd_s, nd_r, "dp", dp, 2 * YS)
    drain(norm_t, nt_s, nt_r, "tensor", ten, TENS)


def hand_over(*refs):
    sems = refs[-1]
    copies = [
        pltpu.make_async_copy(refs[i], refs[8 + i], sems.at[i]) for i in (4, 0, 1, 2, 3, 5, 6, 7)
    ]
    for copy in copies:
        copy.start()
    for copy in copies:
        copy.wait()


def body(grad_proj, grad_conv, param_proj, m_proj, v_proj, ema_proj, param_conv, m_conv, v_conv):
    small = jax.ShapeDtypeStruct((KCONV, CCOL), F32)
    block = jax.ShapeDtypeStruct((BLK, ROWS), F32)
    dma = pltpu.SemaphoreType.DMA
    outs = pl.pallas_call(
        kernel,
        out_shape=(
            block, block, block,
            jax.ShapeDtypeStruct((EROW, D), F32),
            jax.ShapeDtypeStruct((ROWS, D), BF16),
            small, small, small,
        ),
        in_specs=[pl.BlockSpec(memory_space=pltpu.HBM)] * 9,
        out_specs=[pl.BlockSpec(memory_space=pltpu.VMEM)] * 8,
        scratch_shapes=[
            pltpu.VMEM((ROWS, D), F32),
            pltpu.VMEM((D, ROWS), F32),
            pltpu.VMEM((YS, BLK, ROWS), BF16),
            pltpu.VMEM((YS, BLK, ROWS), BF16),
            pltpu.VMEM((2, HALF, ROWS), BF16),
            pltpu.VMEM((2, HALF, ROWS), BF16),
            pltpu.VMEM((2, BLK, ROWS), BF16),
            pltpu.VMEM((2, BLK, ROWS), BF16),
            pltpu.VMEM((4, HALF, ROWS), BF16),
            pltpu.VMEM((4, HALF, ROWS), BF16),
            pltpu.VMEM((2, BLK, ROWS), BF16),
            pltpu.VMEM((2, BLK, ROWS), BF16),
            pltpu.VMEM((2 * REPS, HALF, ROWS), BF16),
            pltpu.VMEM((D, ROWS), BF16),
            pltpu.VMEM((BLK, ROWS), F32),
            pltpu.VMEM((BLK, ROWS), F32),
            pltpu.VMEM((BLK, ROWS), F32),
            pltpu.VMEM((EROW, D), F32),
            pltpu.VMEM((YS, KCONV, CCOL), F32),
            pltpu.VMEM((2, KCONV, CCOL), F32),
            pltpu.VMEM((REPS, KCONV, CCOL), F32),
            pltpu.VMEM((KCONV, CCOL), F32),
            pltpu.VMEM((KCONV, CCOL), F32),
            pltpu.VMEM((KCONV, CCOL), F32),
            pltpu.VMEM((2 * YS, 8, 128), F32),
            pltpu.VMEM((TENS, 8, 128), F32),
            dma((12,)),
            dma((YS,)), dma((YS,)),
            dma((2,)), dma((2,)),
            dma((2,)), dma((2,)),
            dma((4,)), dma((4,)),
            dma((2,)), dma((2,)),
            dma((2 * REPS,)), dma((2 * REPS,)),
            dma((6,)), dma((6,)),
            dma((6,)), dma((6,)),
            dma((2 * YS,)), dma((2 * YS,)),
            dma((YS,)), dma((YS,)),
            dma, dma,
            dma((REPS,)), dma((REPS,)),
            dma((2 * YS,)), dma((2 * YS,)),
            dma((TENS,)), dma((TENS,)),
        ],
        compiler_params=pltpu.CompilerParams(
            collective_id=0, has_side_effects=True, vmem_limit_bytes=48 << 20
        ),
        name="adamw_step",
    )(
        *(
            pltpu.with_memory_space_constraint(x, pltpu.HBM)
            for x in (
                grad_proj[0], grad_conv[0], param_proj.T, m_proj.T, v_proj.T, ema_proj,
                param_conv, m_conv, v_conv,
            )
        )
    )
    outs = pl.pallas_call(
        hand_over,
        out_shape=tuple(jax.ShapeDtypeStruct(x.shape, x.dtype) for x in outs),
        in_specs=[pl.BlockSpec(memory_space=pltpu.VMEM)] * 8,
        out_specs=[pl.BlockSpec(memory_space=pltpu.HBM)] * 8,
        scratch_shapes=[dma((8,))],
        name="hand_over",
    )(*(pltpu.with_memory_space_constraint(x, pltpu.VMEM) for x in outs))
    new_param, new_m, new_v, new_ema, weights, new_cparam, new_cm, new_cv = outs
    return (new_param.T, new_m.T, new_v.T, new_ema, weights, new_cparam, new_cm, new_cv)


def solution(mesh):
    in_specs = (
        P(("rep", "dp"), "tensor", None),
        P(("rep", "dp"), None, "tensor"),
        P("tensor", "dp"),
        P("tensor", "dp"),
        P("tensor", "dp"),
        P(("tensor", "dp"), None),
        P(None, "tensor"),
        P(None, "tensor"),
        P(None, "tensor"),
    )
    out_specs = (
        P("tensor", "dp"),
        P("tensor", "dp"),
        P("tensor", "dp"),
        P(("tensor", "dp"), None),
        P("tensor", None),
        P(None, "tensor"),
        P(None, "tensor"),
        P(None, "tensor"),
    )
    return jax.shard_map(body, mesh=mesh, in_specs=in_specs, out_specs=out_specs, check_vma=False)
```

time: 82.8 us -> 60.8 us (0.73)
  local copies, waits for them, and re-layouts: 13.5 us -> 0 us
  Pallas kernels: 68.2 us -> 60 us
    unnamed x26 -> x0, local copies, waits for them, and re-layouts: 13.5 us -> none
    pallas_call x1, Pallas kernels: 68.2 us -> 58.7 us  [body(): pl.pallas_call(kernel, out_shape=(block, block, block, jax.ShapeDtypeStru...]
    pallas_call x0 -> x1, Pallas kernels: none -> 1.27 us  [body(): pl.pallas_call(hand_over, out_shape=tuple((jax.ShapeDtypeStruct(x.shape,...]
where the time goes in v2:
time: 60.8 us; the launch traced here: 60.6 us
  Pallas kernels  60 us (99%)
  between operations  0.64 us (1%)
    pallas_call x1, Pallas kernels, body(): pl.pallas_call(kernel, out_shape=(block, block, block, jax.ShapeDtypeStru...  58.7 us
    pallas_call x1, Pallas kernels, body(): pl.pallas_call(hand_over, out_shape=tuple((jax.ShapeDtypeStruct(x.shape,...  1.27 us

profile of v2, /device:TPU:1, one launch (start us, length us, event | category | flops | bytes accessed | tf_op | source)
XLA Modules:
  0.0 60.6 jit_solution(3366339707598731961)
XLA Ops:
  0.6 58.7 %adamw_step.1 = (f32[96,384]{1,0:T(8,128)S(1)}, f32[96,384]{1,0:T(8,128)S(1)}, f32[96,384]{1,0:T(8,128)S(1)}, f32[24,1536]{1,0:T(8,128)S(1)}, bf16[384,1536]{1,0...) custom-call(f32[384,1536]{1,0:T(8,128)} %bitcast.8, f32[4,416]{1,0:T(4,128)} %bitcast.12, ...), custom_call_target="tpu_custom_call" | custom-call | tf_op jit(solution)/shard_map/adamw_step/pallas_call | solution.py:450
  59.4 1.3 %hand_over.1 = (f32[96,384]{1,0:T(8,128)}, f32[96,384]{1,0:T(8,128)}, f32[96,384]{1,0:T(8,128)}, f32[24,1536]{1,0:T(8,128)}, bf16[384,1536]{1,0:T(8,128)(2,1)}, ...) custom-call(f32[96,384]{1,0:T(8,128)S(1)} %get-tuple-element.24.refs_0_, ...), custom_call_target="tpu_custom_call" | custom-call | tf_op jit(solution)/shard_map/hand_over/pallas_call | solution.py:516

commit v3 on v2

--- a/solution.py
+++ b/solution.py
@@ -77,7 +77,7 @@
     zx, wt, p_v, m_v, v_v, e_v, conv_y, conv_c, conv_z, cp_v, cm_v, cv_v, norm_d, norm_t,
     load_sem, pair_s, pair_r, far_s, far_r, mid_s, mid_r, rel_s, rel_r, near_s, near_r, zx_s, zx_r,
     own_s, own_r, fwd_s, fwd_r, share_s, share_r, cy_s, cy_r, cc_s, cc_r, cz_s, cz_r,
-    nd_s, nd_r, nt_s, nt_r,
+    nd_s, nd_r, nt_s, nt_r, hello_z, hello_x,
 ):
     rep = lax.axis_index("rep")
     dp = lax.axis_index("dp")
@@ -87,7 +87,7 @@
     partner = 2 * y + (1 - core)
 
     def y_at(off):
-        return (y + (off + YS)) % YS
+        return (y + off + YS) % YS
 
     def remote(src, dst, send, recv, **device):
         return pltpu.make_async_remote_copy(
@@ -102,30 +102,25 @@
     for i, group in enumerate(order):
         cols = pl.ds(pl.multiple_of(group * 384, 128), 384)
         loads.append(pltpu.make_async_copy(grad.at[:, cols], g_in.at[:, cols], load_sem.at[i]))
-        loads[-1].start()
-    conv_load = pltpu.make_async_copy(conv, conv_y.at[y], load_sem.at[4])
-    conv_load.start()
+    for copy in loads:
+        copy.start()
+    conv_load = pltpu.make_async_copy(conv, conv_z.at[rep], load_sem.at[4])
     late = []
     for i, (src, dst) in enumerate(
         ((param, p_v), (mom, m_v), (vel, v_v), (ema, e_v), (cparam, cp_v), (cmom, cm_v), (cvel, cv_v))
     ):
         late.append(pltpu.make_async_copy(src, dst, load_sem.at[5 + i]))
-        late[-1].start()
-
+
+    x_near = [{"tensor": (ten + 2) % TENS}, {"tensor": (ten + TENS - 2) % TENS}, {"tensor": ten + 1 - 2 * (ten % 2)}]
+    z_near = [{"rep": (rep + 1) % REPS}, {"rep": (rep + REPS - 1) % REPS}]
+    y_near = [{"dp": 2 * y_at(off) + core} for off in (2, -2, 1, -1)]
     barrier = pltpu.get_barrier_semaphore()
 
-    def greet(axis, me, count):
-        def step(i, carry):
-            pl.semaphore_signal(
-                barrier, inc=1, device_id={axis: (me + i) % count}, device_id_type=MESH
-            )
-            return carry
-
-        lax.fori_loop(1, count, step, 0)
-
-    greet("dp", dp, 2 * YS)
-    greet("rep", rep, REPS)
-    greet("tensor", ten, TENS)
+    def signal(sem, devices):
+        for device in devices:
+            pl.semaphore_signal(sem, inc=1, device_id=device, device_id_type=MESH)
+
+    signal(barrier, y_near[:2] + z_near + y_near[2:] + x_near + [{"dp": partner}])
 
     def turn_group(i):
         loads[i].wait()
@@ -152,17 +147,16 @@
             conv_y.at[y], conv_y.at[y], cy_s.at[off], cy_r.at[y], dp=2 * y_at(off) + core
         )
 
-    turn_group(0)
-    conv_load.wait()
-    pl.semaphore_wait(barrier, (2 * YS - 1) + (REPS - 1) + (TENS - 1))
-    for k in range(2):
-        pair_copy(2 * order[0] + k).start()
-    for off in range(1, YS):
-        conv_y_copy(off).start()
-    for i in range(1, 4):
+    for copy in [conv_load] + late:
+        copy.start()
+    for i in range(4):
         turn_group(i)
+    pl.semaphore_wait(barrier, 10)
+    for i in range(4):
         for k in range(2):
             pair_copy(2 * order[i] + k).start()
+    signal(hello_z, z_near)
+    signal(hello_x.at[0], x_near)
 
     arrived = set()
 
@@ -181,14 +175,14 @@
     def far_copy(i):
         return y_copy(far_out, far_in, far_s, far_r, i, 2 * WAYS[i][0])
 
-    def mid_copy(i):
-        return y_copy(mid_out, mid_in, mid_s, mid_r, i, WAYS[i][0])
+    def mid_copy(i, half):
+        return y_copy(mid_out, mid_in, mid_s, mid_r, 2 * i + half, WAYS[i][0])
 
     def rel_copy(i, half):
         return y_copy(rel_out, rel_in, rel_s, rel_r, 2 * i + half, 2 * WAYS[i][0])
 
-    def near_copy(i):
-        return y_copy(near_out, near_in, near_s, near_r, i, WAYS[i][0])
+    def near_copy(i, half):
+        return y_copy(near_out, near_in, near_s, near_r, 2 * i + half, WAYS[i][0])
 
     def conv_c_copy():
         return remote(conv_c.at[core], conv_c.at[core], cc_s, cc_r, dp=partner)
@@ -201,40 +195,32 @@
     for i, (sign, half) in enumerate(WAYS):
         far_out[i] = encode(local_sum(4 * sign, half))
         far_copy(i).start()
-    for i, (sign, _) in enumerate(WAYS):
-        mid_out[i] = encode(local_sum(3 * sign))
-        mid_copy(i).start()
-    for i, (sign, _) in enumerate(WAYS):
-        near_out[i] = encode(local_sum(sign))
-        near_copy(i).start()
-
-    for off in range(1, YS):
-        src = y_at(off)
-        remote(conv_y.at[src], conv_y.at[src], cy_s.at[off], cy_r.at[src], dp=partner).wait_recv()
-    total = conv_y[0]
-    for i in range(1, YS):
-        total = total + conv_y[i]
-    conv_c[core] = total
-    conv_c_copy().start()
-    for i, (sign, half) in enumerate(WAYS):
-        mid_copy(i).wait_recv()
-        far_copy(i).wait_recv()
-        for h in (half, 1 - half):
-            total = local_sum(2 * sign, h) + decode(mid_in[i, h * HALF : (h + 1) * HALF, :])
-            if h == half:
-                total = total + decode(far_in[i])
-            rel_out[2 * i + h] = encode(total)
-            rel_copy(i, h).start()
-    conv_c_copy().wait_recv()
-    conv_z[rep] = conv_c[0] + conv_c[1]
+    for h in range(2):
+        for i, (sign, _) in enumerate(WAYS):
+            mid_out[2 * i + h] = encode(local_sum(3 * sign, h))
+            mid_copy(i, h).start()
+    for h in range(2):
+        for i, (sign, _) in enumerate(WAYS):
+            near_out[2 * i + h] = encode(local_sum(sign, h))
+    for i in range(2):
+        mid_copy(i, 1).wait_send()
+    for h in range(2):
+        for i in range(2):
+            near_copy(i, h).start()
+    for i, h in ((0, 0), (1, 0), (1, 1), (0, 1)):
+        mid_copy(i, h).wait_recv()
+        total = local_sum(2 * WAYS[i][0], h) + decode(mid_in[2 * i + h])
+        if h == WAYS[i][1]:
+            far_copy(i).wait_recv()
+            total = total + decode(far_in[i])
+        rel_out[2 * i + h] = encode(total)
+        rel_copy(i, h).start()
+    conv_load.wait()
+    pl.semaphore_wait(hello_z, 2)
     for off in range(1, REPS):
         conv_z_copy(off).start()
-
-    mine_sum = [local_sum(0, h) for h in range(2)]
-    for i in range(2):
-        near_copy(i).wait_recv()
-        for h in range(2):
-            mine_sum[h] = mine_sum[h] + decode(near_in[i, h * HALF : (h + 1) * HALF, :])
+    pl.semaphore_wait(hello_x.at[0], 3)
+    signal(hello_x.at[1], x_near)
 
     def zx_copy(off, h):
         return remote(
@@ -243,19 +229,24 @@
         )
 
     for h in range(2):
+        total = local_sum(0, h)
+        for i in range(2):
+            near_copy(i, h).wait_recv()
+            total = total + decode(near_in[2 * i + h])
         for i in range(2):
             rel_copy(i, h).wait_recv()
-            mine_sum[h] = mine_sum[h] + decode(rel_in[2 * i + h])
-        zx[2 * rep + h] = encode(mine_sum[h])
+            total = total + decode(rel_in[2 * i + h])
+        zx[2 * rep + h] = encode(total)
         for off in (2, 1, 3):
             zx_copy(off, h).start()
 
+    count = float(REPS * 2 * YS)
     for off in range(1, REPS):
         src = (rep + off) % REPS
         remote(conv_z.at[src], conv_z.at[src], cz_s.at[off], cz_r.at[src], dp=partner).wait_recv()
-    count = float(REPS * 2 * YS)
-    conv_avg = (((conv_z[0] + conv_z[1]) + conv_z[2]) + conv_z[3]) * (1.0 / count)
-    conv_square = jnp.sum(conv_avg * conv_avg)
+    conv_y[y] = ((conv_z[0] + conv_z[1]) + conv_z[2]) + conv_z[3]
+    for off in range(1, YS):
+        conv_y_copy(off).start()
 
     avg = []
     for h in range(2):
@@ -266,6 +257,15 @@
         for r in range(1, REPS):
             total = total + decode(zx[2 * r + h])
         avg.append(total * (1.0 / count))
+        if h == 0:
+            for off in range(1, YS):
+                src = y_at(off)
+                remote(conv_y.at[src], conv_y.at[src], cy_s.at[off], cy_r.at[src], dp=partner).wait_recv()
+            total = conv_y[0]
+            for i in range(1, YS):
+                total = total + conv_y[i]
+            conv_c[core] = total
+            conv_c_copy().start()
 
     def row_copy(buf, send, recv, axis, me, i, size):
         to = (me + i) % size
@@ -306,6 +306,10 @@
         gt[h * HALF : (h + 1) * HALF, :] = avg[h]
     for copy in late:
         copy.wait()
+    conv_c_copy().wait_recv()
+    conv_avg = (conv_c[0] + conv_c[1]) * (1.0 / count)
+    conv_square = jnp.sum(conv_avg * conv_avg)
+    pl.semaphore_wait(hello_x.at[1], 3)
     norm_t[ten, 0:1, :] = collect(norm_d, nd_s, nd_r, "dp", dp, 2 * YS) + conv_square * (1.0 / 128.0)
     spread(norm_t, nt_s, nt_r, "tensor", ten, TENS)
 
@@ -347,8 +351,6 @@
     for k in range(2):
         for i, (sign, half) in enumerate(WAYS):
             own2_copy(i, half if k == 0 else 1 - half).start()
-    for i in range(2):
-        own1_copy(i).start()
     share_copy(0, None, core).start()
 
     o_param[...] = new_param
@@ -358,6 +360,30 @@
     o_cparam[...] = new_cparam
     o_cmom[...] = new_cmom
     o_cvel[...] = new_cvel
+
+    for h in range(2):
+        for i in range(2):
+            own2_copy(i, h).wait_send()
+    for i in range(2):
+        own1_copy(i).start()
+
+    for off in range(YS):
+        pair_copy(y_at(off)).wait_send()
+    for i in range(2):
+        far_copy(i).wait_send()
+        mid_copy(i, 0).wait_send()
+        for h in range(2):
+            near_copy(i, h).wait_send()
+            rel_copy(i, h).wait_send()
+    for off in range(1, YS):
+        conv_y_copy(off).wait_send()
+    conv_c_copy().wait_send()
+    for off in range(1, REPS):
+        conv_z_copy(off).wait_send()
+        for h in range(2):
+            zx_copy(off, h).wait_send()
+    drain(norm_d, nd_s, nd_r, "dp", dp, 2 * YS)
+    drain(norm_t, nt_s, nt_r, "tensor", ten, TENS)
 
     for k in range(2):
         for i, (sign, half) in enumerate(WAYS):
@@ -395,41 +421,27 @@
             h = half if k == 0 else 1 - half
             fwd1_copy(i, h).wait_recv()
             share_copy(-3 * sign, h, core).start()
-    for off in (4, 3, -3):
+    for h in range(2):
+        share_copy(-3 * turn, h, 1 - core).wait_recv()
+    back(2 * ((pair - turn + 4) % 4))
+    for off in (4, 3 * turn):
         for h in range(2):
             share_copy(off, h, 1 - core).wait_recv()
-    back(2 * ((pair - turn + 4) % 4))
     back(2 * ((pair + 2) % 4))
     near = o_weights[pl.ds(pl.multiple_of(y * 2 * EROW, 16), 2 * EROW), :].astype(F32)
     row_block = jnp.where(core == 0, near[0:EROW], near[EROW:])
     o_ema[...] = 0.9 * e_v[...] + 0.1 * row_block
 
-    for off in range(YS):
-        pair_copy(y_at(off)).wait_send()
     for i, (sign, half) in enumerate(WAYS):
-        far_copy(i).wait_send()
-        mid_copy(i).wait_send()
-        near_copy(i).wait_send()
         own1_copy(i).wait_send()
         fwd2_copy(i).wait_send()
         share_copy(-sign, None, core).wait_send()
         share_copy(-4 * sign, half, core).wait_send()
         for h in range(2):
-            rel_copy(i, h).wait_send()
-            own2_copy(i, h).wait_send()
             fwd1_copy(i, h).wait_send()
             share_copy(-2 * sign, h, core).wait_send()
             share_copy(-3 * sign, h, core).wait_send()
     share_copy(0, None, core).wait_send()
-    for off in range(1, YS):
-        conv_y_copy(off).wait_send()
-    conv_c_copy().wait_send()
-    for off in range(1, REPS):
-        conv_z_copy(off).wait_send()
-        for h in range(2):
-            zx_copy(off, h).wait_send()
-    drain(norm_d, nd_s, nd_r, "dp", dp, 2 * YS)
-    drain(norm_t, nt_s, nt_r, "tensor", ten, TENS)
 
 
 def hand_over(*refs):
@@ -464,12 +476,12 @@
             pltpu.VMEM((YS, BLK, ROWS), BF16),
             pltpu.VMEM((2, HALF, ROWS), BF16),
             pltpu.VMEM((2, HALF, ROWS), BF16),
-            pltpu.VMEM((2, BLK, ROWS), BF16),
-            pltpu.VMEM((2, BLK, ROWS), BF16),
             pltpu.VMEM((4, HALF, ROWS), BF16),
             pltpu.VMEM((4, HALF, ROWS), BF16),
-            pltpu.VMEM((2, BLK, ROWS), BF16),
-            pltpu.VMEM((2, BLK, ROWS), BF16),
+            pltpu.VMEM((4, HALF, ROWS), BF16),
+            pltpu.VMEM((4, HALF, ROWS), BF16),
+            pltpu.VMEM((4, HALF, ROWS), BF16),
+            pltpu.VMEM((4, HALF, ROWS), BF16),
             pltpu.VMEM((2 * REPS, HALF, ROWS), BF16),
             pltpu.VMEM((D, ROWS), BF16),
             pltpu.VMEM((BLK, ROWS), F32),
@@ -487,9 +499,9 @@
             dma((12,)),
             dma((YS,)), dma((YS,)),
             dma((2,)), dma((2,)),
-            dma((2,)), dma((2,)),
             dma((4,)), dma((4,)),
-            dma((2,)), dma((2,)),
+            dma((4,)), dma((4,)),
+            dma((4,)), dma((4,)),
             dma((2 * REPS,)), dma((2 * REPS,)),
             dma((6,)), dma((6,)),
             dma((6,)), dma((6,)),
@@ -499,6 +511,7 @@
             dma((REPS,)), dma((REPS,)),
             dma((2 * YS,)), dma((2 * YS,)),
             dma((TENS,)), dma((TENS,)),
+            pltpu.SemaphoreType.REGULAR, pltpu.SemaphoreType.REGULAR((2,)),
         ],
         compiler_params=pltpu.CompilerParams(
             collective_id=0, has_side_effects=True, vmem_limit_bytes=48 << 20

time: 60.8 us -> 59.9 us (0.985)
  Pallas kernels: 60 us -> 59.1 us
    pallas_call x1, Pallas kernels: 58.7 us -> 57.9 us  [body(): pl.pallas_call(kernel, out_shape=(block, block, block, jax.ShapeDtypeStru...]
where the time goes in v3:
time: 59.9 us; the launch traced here: 59.8 us
  Pallas kernels  59.1 us (99%)
  between operations  0.64 us (1%)
    pallas_call x1, Pallas kernels, body(): pl.pallas_call(kernel, out_shape=(block, block, block, jax.ShapeDtypeStru...  57.9 us
    pallas_call x1, Pallas kernels, body(): pl.pallas_call(hand_over, out_shape=tuple((jax.ShapeDtypeStruct(x.shape,...  1.27 us

profile of v3, /device:TPU:1, one launch (start us, length us, event | category | flops | bytes accessed | tf_op | source)
XLA Modules:
  0.0 59.8 jit_solution(17200930560588940036)
XLA Ops:
  0.6 57.9 %adamw_step.1 = (f32[96,384]{1,0:T(8,128)S(1)}, f32[96,384]{1,0:T(8,128)S(1)}, f32[96,384]{1,0:T(8,128)S(1)}, f32[24,1536]{1,0:T(8,128)S(1)}, bf16[384,1536]{1,0...) custom-call(f32[384,1536]{1,0:T(8,128)} %bitcast.8, f32[4,416]{1,0:T(4,128)} %bitcast.12, ...), custom_call_target="tpu_custom_call" | custom-call | tf_op jit(solution)/shard_map/adamw_step/pallas_call | solution.py:462
  58.5 1.3 %hand_over.1 = (f32[96,384]{1,0:T(8,128)}, f32[96,384]{1,0:T(8,128)}, f32[96,384]{1,0:T(8,128)}, f32[24,1536]{1,0:T(8,128)}, bf16[384,1536]{1,0:T(8,128)(2,1)}, ...) custom-call(f32[96,384]{1,0:T(8,128)S(1)} %get-tuple-element.24.refs_0_, ...), custom_call_target="tpu_custom_call" | custom-call | tf_op jit(solution)/shard_map/hand_over/pallas_call | solution.py:529

commit v4 on v3

--- a/solution.py
+++ b/solution.py
@@ -75,7 +75,7 @@
     o_param, o_mom, o_vel, o_ema, o_weights, o_cparam, o_cmom, o_cvel,
     g_in, gt, pair_out, pair_in, far_out, far_in, mid_out, mid_in, rel_out, rel_in, near_out, near_in,
     zx, wt, p_v, m_v, v_v, e_v, conv_y, conv_c, conv_z, cp_v, cm_v, cv_v, norm_d, norm_t,
-    load_sem, pair_s, pair_r, far_s, far_r, mid_s, mid_r, rel_s, rel_r, near_s, near_r, zx_s, zx_r,
+    load_sem, pair_s, pair_r, step_s, mid_s, far_r, mid_r, rel_r, near_r, zx_s, zx_r,
     own_s, own_r, fwd_s, fwd_r, share_s, share_r, cy_s, cy_r, cc_s, cc_r, cz_s, cz_r,
     nd_s, nd_r, nt_s, nt_r, hello_z, hello_x,
 ):
@@ -94,6 +94,15 @@
             src_ref=src, dst_ref=dst, send_sem=send, recv_sem=recv,
             device_id=device, device_id_type=MESH,
         )
+
+    def sent(ref, sem):
+        remote(ref, ref, sem, cc_r, dp=partner).wait_send()
+
+    def landed(ref, sem):
+        remote(ref, ref, cc_s, sem, dp=partner).wait_recv()
+
+    def wt_rows(n):
+        return wt.at[pl.ds(0, n), :]
 
     base = (y // 2 + 2) % 4
     turn = 2 * (y % 2) - 1
@@ -139,12 +148,12 @@
 
     def pair_copy(own):
         return remote(
-            pair_out.at[own], pair_in.at[own], pair_s.at[own], pair_r.at[own], dp=partner
+            pair_out.at[own], pair_in.at[own], pair_s, pair_r.at[own], dp=partner
         )
 
     def conv_y_copy(off):
         return remote(
-            conv_y.at[y], conv_y.at[y], cy_s.at[off], cy_r.at[y], dp=2 * y_at(off) + core
+            conv_y.at[y], conv_y.at[y], cy_s, cy_r, dp=2 * y_at(off) + core
         )
 
     for copy in [conv_load] + late:
@@ -152,9 +161,12 @@
     for i in range(4):
         turn_group(i)
     pl.semaphore_wait(barrier, 10)
-    for i in range(4):
-        for k in range(2):
-            pair_copy(2 * order[i] + k).start()
+    def pair_start(groups):
+        for i in groups:
+            for k in range(2):
+                pair_copy(2 * order[i] + k).start()
+
+    pair_start((0, 1))
     signal(hello_z, z_near)
     signal(hello_x.at[0], x_near)
 
@@ -169,27 +181,28 @@
         rows = pl.ds(pl.multiple_of((2 * own + core) * BLK + lo, 16), n)
         return gt[rows, :] + decode(pair_in[own, lo : lo + n, :])
 
-    def y_copy(out, into, send, recv, i, hops):
-        return remote(out.at[i], into.at[i], send.at[i], recv.at[i], dp=2 * y_at(hops) + core)
+    def y_copy(out, into, i, send, recv, hops):
+        return remote(out.at[i], into.at[i], send, recv, dp=2 * y_at(hops) + core)
 
     def far_copy(i):
-        return y_copy(far_out, far_in, far_s, far_r, i, 2 * WAYS[i][0])
+        return y_copy(far_out, far_in, i, step_s, far_r.at[i], 2 * WAYS[i][0])
 
     def mid_copy(i, half):
-        return y_copy(mid_out, mid_in, mid_s, mid_r, 2 * i + half, WAYS[i][0])
+        send = mid_s if half else step_s
+        return y_copy(mid_out, mid_in, 2 * i + half, send, mid_r.at[2 * i + half], WAYS[i][0])
 
     def rel_copy(i, half):
-        return y_copy(rel_out, rel_in, rel_s, rel_r, 2 * i + half, 2 * WAYS[i][0])
+        return y_copy(rel_out, rel_in, 2 * i + half, step_s, rel_r.at[half], 2 * WAYS[i][0])
 
     def near_copy(i, half):
-        return y_copy(near_out, near_in, near_s, near_r, 2 * i + half, WAYS[i][0])
+        return y_copy(near_out, near_in, 2 * i + half, step_s, near_r.at[half], WAYS[i][0])
 
     def conv_c_copy():
         return remote(conv_c.at[core], conv_c.at[core], cc_s, cc_r, dp=partner)
 
     def conv_z_copy(off):
         return remote(
-            conv_z.at[rep], conv_z.at[rep], cz_s.at[off], cz_r.at[rep], rep=(rep + off) % REPS
+            conv_z.at[rep], conv_z.at[rep], cz_s, cz_r, rep=(rep + off) % REPS
         )
 
     for i, (sign, half) in enumerate(WAYS):
@@ -199,11 +212,11 @@
         for i, (sign, _) in enumerate(WAYS):
             mid_out[2 * i + h] = encode(local_sum(3 * sign, h))
             mid_copy(i, h).start()
+    pair_start((2, 3))
     for h in range(2):
         for i, (sign, _) in enumerate(WAYS):
             near_out[2 * i + h] = encode(local_sum(sign, h))
-    for i in range(2):
-        mid_copy(i, 1).wait_send()
+    sent(wt_rows(2 * HALF), mid_s)
     for h in range(2):
         for i in range(2):
             near_copy(i, h).start()
@@ -224,80 +237,60 @@
 
     def zx_copy(off, h):
         return remote(
-            zx.at[2 * rep + h], zx.at[2 * rep + h], zx_s.at[2 * off + h], zx_r.at[2 * rep + h],
+            zx.at[2 * rep + h], zx.at[2 * rep + h], zx_s, zx_r.at[h],
             rep=(rep + off) % REPS,
         )
 
     for h in range(2):
         total = local_sum(0, h)
+        landed(near_in.at[pl.ds(0, 2)], near_r.at[h])
         for i in range(2):
-            near_copy(i, h).wait_recv()
             total = total + decode(near_in[2 * i + h])
+        landed(rel_in.at[pl.ds(0, 2)], rel_r.at[h])
         for i in range(2):
-            rel_copy(i, h).wait_recv()
             total = total + decode(rel_in[2 * i + h])
         zx[2 * rep + h] = encode(total)
         for off in (2, 1, 3):
             zx_copy(off, h).start()
 
     count = float(REPS * 2 * YS)
-    for off in range(1, REPS):
-        src = (rep + off) % REPS
-        remote(conv_z.at[src], conv_z.at[src], cz_s.at[off], cz_r.at[src], dp=partner).wait_recv()
+    landed(conv_z.at[pl.ds(0, REPS - 1)], cz_r)
     conv_y[y] = ((conv_z[0] + conv_z[1]) + conv_z[2]) + conv_z[3]
     for off in range(1, YS):
         conv_y_copy(off).start()
 
     avg = []
     for h in range(2):
-        for off in range(1, REPS):
-            src = 2 * ((rep + off) % REPS) + h
-            remote(zx.at[src], zx.at[src], zx_s.at[2 * off + h], zx_r.at[src], dp=partner).wait_recv()
+        landed(zx.at[pl.ds(0, REPS - 1)], zx_r.at[h])
         total = decode(zx[h])
         for r in range(1, REPS):
             total = total + decode(zx[2 * r + h])
         avg.append(total * (1.0 / count))
         if h == 0:
-            for off in range(1, YS):
-                src = y_at(off)
-                remote(conv_y.at[src], conv_y.at[src], cy_s.at[off], cy_r.at[src], dp=partner).wait_recv()
+            landed(conv_y.at[pl.ds(0, YS - 1)], cy_r)
             total = conv_y[0]
             for i in range(1, YS):
                 total = total + conv_y[i]
             conv_c[core] = total
             conv_c_copy().start()
 
-    def row_copy(buf, send, recv, axis, me, i, size):
-        to = (me + i) % size
-        at = buf.at[me, pl.ds(0, 1), :]
-        return remote(at, at, send.at[i], recv.at[me], **{axis: to})
+    def rows_at(buf, first, n):
+        return buf.at[pl.ds(first, n), pl.ds(0, 1), :]
 
     def spread(buf, send, recv, axis, me, size):
         def start(i, carry):
-            row_copy(buf, send, recv, axis, me, i, size).start()
+            at = rows_at(buf, me, 1)
+            remote(at, at, send, recv, **{axis: (me + i) % size}).start()
             return carry
 
         lax.fori_loop(1, size, start, 0)
 
-    def collect(buf, send, recv, axis, me, size):
-        def wait(i, carry):
-            src = (me + i) % size
-            at = buf.at[src, pl.ds(0, 1), :]
-            remote(at, at, send.at[i], recv.at[src], **{axis: src}).wait_recv()
-            return carry
-
-        lax.fori_loop(1, size, wait, 0)
+    def collect(buf, recv, size):
+        landed(rows_at(buf, 0, size - 1), recv)
         total = buf[0, 0:1, :]
         for i in range(1, size):
             total = total + buf[i, 0:1, :]
         return total
-
-    def drain(buf, send, recv, axis, me, size):
-        def wait(i, carry):
-            row_copy(buf, send, recv, axis, me, i, size).wait_send()
-            return carry
-
-        lax.fori_loop(1, size, wait, 0)
 
     square = fold(avg[0] * avg[0]) + fold(avg[1] * avg[1])
     norm_d[dp, 0:1, :] = jnp.sum(square, axis=0, keepdims=True)
@@ -310,10 +303,10 @@
     conv_avg = (conv_c[0] + conv_c[1]) * (1.0 / count)
     conv_square = jnp.sum(conv_avg * conv_avg)
     pl.semaphore_wait(hello_x.at[1], 3)
-    norm_t[ten, 0:1, :] = collect(norm_d, nd_s, nd_r, "dp", dp, 2 * YS) + conv_square * (1.0 / 128.0)
+    norm_t[ten, 0:1, :] = collect(norm_d, nd_r, 2 * YS) + conv_square * (1.0 / 128.0)
     spread(norm_t, nt_s, nt_r, "tensor", ten, TENS)
 
-    square_sum = jnp.sum(collect(norm_t, nt_s, nt_r, "tensor", ten, TENS), keepdims=True)
+    square_sum = jnp.sum(collect(norm_t, nt_r, TENS), keepdims=True)
     clip = clip_from(square_sum)
 
     new_param, new_mom, new_vel = adamw_step(p_v[...], m_v[...], v_v[...], clip * gt[0:BLK, :])
@@ -327,14 +320,14 @@
     def gather_copy(send, recv, slot, off, half, hops):
         rows = rows_of(off, core, half)
         return remote(
-            wt.at[rows, :], wt.at[rows, :], send.at[slot], recv.at[slot], dp=2 * y_at(hops) + core
+            wt.at[rows, :], wt.at[rows, :], send, recv.at[slot], dp=2 * y_at(hops) + core
         )
 
     def own2_copy(i, half):
         return gather_copy(own_s, own_r, 2 * i + half, 0, half, 2 * WAYS[i][0])
 
     def own1_copy(i):
-        return gather_copy(own_s, own_r, 4 + i, 0, None, WAYS[i][0])
+        return gather_copy(fwd_s, own_r, 4 + i, 0, None, WAYS[i][0])
 
     def fwd1_copy(i, half):
         return gather_copy(fwd_s, fwd_r, 2 * i + half, -2 * WAYS[i][0], half, WAYS[i][0])
@@ -343,15 +336,15 @@
         sign, half = WAYS[i]
         return gather_copy(fwd_s, fwd_r, 4 + i, -2 * sign, half, 2 * sign)
 
-    def share_copy(off, half, whose):
-        rows = rows_of(off, whose, half)
-        slot = 2 * y_at(off) + (half or 0)
-        return remote(wt.at[rows, :], wt.at[rows, :], share_s.at[slot], share_r.at[slot], dp=partner)
+    def share_copy(off, half):
+        rows = rows_of(off, core, half)
+        slot = 0 if abs(off) <= 2 else 2 if off == 4 else (3 - turn * (-off // 3)) // 2
+        return remote(wt.at[rows, :], wt.at[rows, :], share_s, share_r.at[slot], dp=partner)
 
     for k in range(2):
         for i, (sign, half) in enumerate(WAYS):
             own2_copy(i, half if k == 0 else 1 - half).start()
-    share_copy(0, None, core).start()
+    share_copy(0, None).start()
 
     o_param[...] = new_param
     o_mom[...] = new_mom
@@ -361,29 +354,18 @@
     o_cmom[...] = new_cmom
     o_cvel[...] = new_cvel
 
-    for h in range(2):
-        for i in range(2):
-            own2_copy(i, h).wait_send()
+    sent(wt_rows(4 * HALF), own_s)
     for i in range(2):
         own1_copy(i).start()
 
-    for off in range(YS):
-        pair_copy(y_at(off)).wait_send()
-    for i in range(2):
-        far_copy(i).wait_send()
-        mid_copy(i, 0).wait_send()
-        for h in range(2):
-            near_copy(i, h).wait_send()
-            rel_copy(i, h).wait_send()
-    for off in range(1, YS):
-        conv_y_copy(off).wait_send()
+    sent(pair_out, pair_s)
+    sent(wt_rows(12 * HALF), step_s)
+    sent(conv_y.at[pl.ds(0, YS - 1)], cy_s)
     conv_c_copy().wait_send()
-    for off in range(1, REPS):
-        conv_z_copy(off).wait_send()
-        for h in range(2):
-            zx_copy(off, h).wait_send()
-    drain(norm_d, nd_s, nd_r, "dp", dp, 2 * YS)
-    drain(norm_t, nt_s, nt_r, "tensor", ten, TENS)
+    sent(conv_z.at[pl.ds(0, REPS - 1)], cz_s)
+    sent(zx.at[pl.ds(0, 2 * (REPS - 1))], zx_s)
+    sent(rows_at(norm_d, 0, 2 * YS - 1), nd_s)
+    sent(rows_at(norm_t, 0, TENS - 1), nt_s)
 
     for k in range(2):
         for i, (sign, half) in enumerate(WAYS):
@@ -392,56 +374,41 @@
             if k == 0:
                 fwd2_copy(i).start()
             fwd1_copy(i, h).start()
-            share_copy(-2 * sign, h, core).start()
+            share_copy(-2 * sign, h).start()
     for i, (sign, _) in enumerate(WAYS):
         own1_copy(i).wait_recv()
-        share_copy(-sign, None, core).start()
+        share_copy(-sign, None).start()
 
     def back(first):
         def step(j, carry):
             at = pl.multiple_of(first * 192 + j * 128, 128)
-            o_weights[:, pl.ds(at, 128)] = wt[pl.ds(at, 128), :].astype(F32).T.astype(BF16)
+            o_weights[:, pl.ds(at, 128)] = wt[pl.ds(at, 128), :].T
             return carry
 
         lax.fori_loop(0, 3, step, 0)
 
-    share_copy(0, None, 1 - core).wait_recv()
-    for sign, _ in WAYS:
-        share_copy(-sign, None, 1 - core).wait_recv()
-        for h in range(2):
-            share_copy(-2 * sign, h, 1 - core).wait_recv()
-    pair = y // 2
-    back(2 * pair)
-    back(2 * ((pair + turn + 4) % 4))
     for i, (sign, half) in enumerate(WAYS):
         fwd2_copy(i).wait_recv()
-        share_copy(-4 * sign, half, core).start()
+        share_copy(4, half).start()
     for k in range(2):
         for i, (sign, half) in enumerate(WAYS):
             h = half if k == 0 else 1 - half
             fwd1_copy(i, h).wait_recv()
-            share_copy(-3 * sign, h, core).start()
-    for h in range(2):
-        share_copy(-3 * turn, h, 1 - core).wait_recv()
+            share_copy(-3 * sign, h).start()
+    landed(wt_rows(5 * BLK), share_r.at[0])
+    pair = y // 2
+    back(2 * pair)
+    back(2 * ((pair + turn + 4) % 4))
+    landed(wt_rows(BLK), share_r.at[1])
     back(2 * ((pair - turn + 4) % 4))
-    for off in (4, 3 * turn):
-        for h in range(2):
-            share_copy(off, h, 1 - core).wait_recv()
+    landed(wt_rows(2 * BLK), share_r.at[2])
     back(2 * ((pair + 2) % 4))
     near = o_weights[pl.ds(pl.multiple_of(y * 2 * EROW, 16), 2 * EROW), :].astype(F32)
     row_block = jnp.where(core == 0, near[0:EROW], near[EROW:])
     o_ema[...] = 0.9 * e_v[...] + 0.1 * row_block
 
-    for i, (sign, half) in enumerate(WAYS):
-        own1_copy(i).wait_send()
-        fwd2_copy(i).wait_send()
-        share_copy(-sign, None, core).wait_send()
-        share_copy(-4 * sign, half, core).wait_send()
-        for h in range(2):
-            fwd1_copy(i, h).wait_send()
-            share_copy(-2 * sign, h, core).wait_send()
-            share_copy(-3 * sign, h, core).wait_send()
-    share_copy(0, None, core).wait_send()
+    sent(wt_rows(10 * HALF), fwd_s)
+    sent(wt_rows(8 * BLK), share_s)
 
 
 def hand_over(*refs):
@@ -497,20 +464,18 @@
             pltpu.VMEM((2 * YS, 8, 128), F32),
             pltpu.VMEM((TENS, 8, 128), F32),
             dma((12,)),
-            dma((YS,)), dma((YS,)),
-            dma((2,)), dma((2,)),
-            dma((4,)), dma((4,)),
-            dma((4,)), dma((4,)),
-            dma((4,)), dma((4,)),
-            dma((2 * REPS,)), dma((2 * REPS,)),
-            dma((6,)), dma((6,)),
-            dma((6,)), dma((6,)),
-            dma((2 * YS,)), dma((2 * YS,)),
-            dma((YS,)), dma((YS,)),
+            dma, dma((YS,)),
             dma, dma,
-            dma((REPS,)), dma((REPS,)),
-            dma((2 * YS,)), dma((2 * YS,)),
-            dma((TENS,)), dma((TENS,)),
+            dma((2,)), dma((4,)), dma((2,)), dma((2,)),
+            dma, dma((2,)),
+            dma, dma((6,)),
+            dma, dma((6,)),
+            dma, dma((3,)),
+            dma, dma,
+            dma, dma,
+            dma, dma,
+            dma, dma,
+            dma, dma,
             pltpu.SemaphoreType.REGULAR, pltpu.SemaphoreType.REGULAR((2,)),
         ],
         compiler_params=pltpu.CompilerParams(

time: 59.9 us -> 58.6 us (0.978)
  Pallas kernels: 59.1 us -> 57.8 us
    pallas_call x1, Pallas kernels: 57.9 us -> 56.5 us  [body(): pl.pallas_call(kernel, out_shape=(block, block, block, jax.ShapeDtypeStru...]
where the time goes in v4:
time: 58.6 us; the launch traced here: 58.4 us
  Pallas kernels  57.8 us (99%)
  between operations  0.64 us (1%)
    pallas_call x1, Pallas kernels, body(): pl.pallas_call(kernel, out_shape=(block, block, block, jax.ShapeDtypeStru...  56.5 us
    pallas_call x1, Pallas kernels, body(): pl.pallas_call(hand_over, out_shape=tuple((jax.ShapeDtypeStruct(x.shape,...  1.27 us

profile of v4, /device:TPU:1, one launch (start us, length us, event | category | flops | bytes accessed | tf_op | source)
XLA Modules:
  0.0 58.4 jit_solution(5534967925613748670)
XLA Ops:
  0.6 56.5 %adamw_step.1 = (f32[96,384]{1,0:T(8,128)S(1)}, f32[96,384]{1,0:T(8,128)S(1)}, f32[96,384]{1,0:T(8,128)S(1)}, f32[24,1536]{1,0:T(8,128)S(1)}, bf16[384,1536]{1,0...) custom-call(f32[384,1536]{1,0:T(8,128)} %bitcast.8, f32[4,416]{1,0:T(4,128)} %bitcast.12, ...), custom_call_target="tpu_custom_call" | custom-call | tf_op jit(solution)/shard_map/adamw_step/pallas_call | solution.py:429
  57.1 1.3 %hand_over.1 = (f32[96,384]{1,0:T(8,128)}, f32[96,384]{1,0:T(8,128)}, f32[96,384]{1,0:T(8,128)}, f32[24,1536]{1,0:T(8,128)}, bf16[384,1536]{1,0:T(8,128)(2,1)}, ...) custom-call(f32[96,384]{1,0:T(8,128)S(1)} %get-tuple-element.24.refs_0_, ...), custom_call_target="tpu_custom_call" | custom-call | tf_op jit(solution)/shard_map/hand_over/pallas_call | solution.py:494

commit v5 on v4

--- a/solution.py
+++ b/solution.py
@@ -74,8 +74,8 @@
     grad, conv, param, mom, vel, ema, cparam, cmom, cvel,
     o_param, o_mom, o_vel, o_ema, o_weights, o_cparam, o_cmom, o_cvel,
     g_in, gt, pair_out, pair_in, far_out, far_in, mid_out, mid_in, rel_out, rel_in, near_out, near_in,
-    zx, wt, p_v, m_v, v_v, e_v, conv_y, conv_c, conv_z, cp_v, cm_v, cv_v, norm_d, norm_t,
-    load_sem, pair_s, pair_r, step_s, mid_s, far_r, mid_r, rel_r, near_r, zx_s, zx_r,
+    zx, wt, state, e_v, conv_y, conv_c, conv_z, cstate, norm_d, norm_t,
+    load_sem, pair_s, pair_r, step_s, mid_s, mid_r, rel_r, near_r, zx_s, zx_r,
     own_s, own_r, fwd_s, fwd_r, share_s, share_r, cy_s, cy_r, cc_s, cc_r, cz_s, cz_r,
     nd_s, nd_r, nt_s, nt_r, hello_z, hello_x,
 ):
@@ -115,10 +115,11 @@
         copy.start()
     conv_load = pltpu.make_async_copy(conv, conv_z.at[rep], load_sem.at[4])
     late = []
-    for i, (src, dst) in enumerate(
-        ((param, p_v), (mom, m_v), (vel, v_v), (ema, e_v), (cparam, cp_v), (cmom, cm_v), (cvel, cv_v))
+    for src, dst, i in (
+        (param, state.at[0], 5), (mom, state.at[1], 5), (vel, state.at[2], 5), (ema, e_v, 6),
+        (cparam, cstate.at[0], 7), (cmom, cstate.at[1], 7), (cvel, cstate.at[2], 7),
     ):
-        late.append(pltpu.make_async_copy(src, dst, load_sem.at[5 + i]))
+        late.append(pltpu.make_async_copy(src, dst, load_sem.at[i]))
 
     x_near = [{"tensor": (ten + 2) % TENS}, {"tensor": (ten + TENS - 2) % TENS}, {"tensor": ten + 1 - 2 * (ten % 2)}]
     z_near = [{"rep": (rep + 1) % REPS}, {"rep": (rep + REPS - 1) % REPS}]
@@ -185,11 +186,11 @@
         return remote(out.at[i], into.at[i], send, recv, dp=2 * y_at(hops) + core)
 
     def far_copy(i):
-        return y_copy(far_out, far_in, i, step_s, far_r.at[i], 2 * WAYS[i][0])
+        return y_copy(far_out, far_in, i, step_s, mid_r.at[i], 2 * WAYS[i][0])
 
     def mid_copy(i, half):
         send = mid_s if half else step_s
-        return y_copy(mid_out, mid_in, 2 * i + half, send, mid_r.at[2 * i + half], WAYS[i][0])
+        return y_copy(mid_out, mid_in, 2 * i + half, send, mid_r.at[half], WAYS[i][0])
 
     def rel_copy(i, half):
         return y_copy(rel_out, rel_in, 2 * i + half, step_s, rel_r.at[half], 2 * WAYS[i][0])
@@ -221,10 +222,10 @@
         for i in range(2):
             near_copy(i, h).start()
     for i, h in ((0, 0), (1, 0), (1, 1), (0, 1)):
-        mid_copy(i, h).wait_recv()
+        if i == h:
+            landed(wt_rows(3 * HALF), mid_r.at[h])
         total = local_sum(2 * WAYS[i][0], h) + decode(mid_in[2 * i + h])
         if h == WAYS[i][1]:
-            far_copy(i).wait_recv()
             total = total + decode(far_in[i])
         rel_out[2 * i + h] = encode(total)
         rel_copy(i, h).start()
@@ -278,12 +279,9 @@
         return buf.at[pl.ds(first, n), pl.ds(0, 1), :]
 
     def spread(buf, send, recv, axis, me, size):
-        def start(i, carry):
-            at = rows_at(buf, me, 1)
+        at = rows_at(buf, me, 1)
+        for i in sorted(range(1, size), key=lambda i: abs(i - size // 2)):
             remote(at, at, send, recv, **{axis: (me + i) % size}).start()
-            return carry
-
-        lax.fori_loop(1, size, start, 0)
 
     def collect(buf, recv, size):
         landed(rows_at(buf, 0, size - 1), recv)
@@ -297,8 +295,8 @@
     spread(norm_d, nd_s, nd_r, "dp", dp, 2 * YS)
     for h in range(2):
         gt[h * HALF : (h + 1) * HALF, :] = avg[h]
-    for copy in late:
-        copy.wait()
+    for ref, i in ((state, 5), (e_v, 6), (cstate, 7)):
+        pltpu.make_async_copy(ref, ref, load_sem.at[i]).wait()
     conv_c_copy().wait_recv()
     conv_avg = (conv_c[0] + conv_c[1]) * (1.0 / count)
     conv_square = jnp.sum(conv_avg * conv_avg)
@@ -309,7 +307,7 @@
     square_sum = jnp.sum(collect(norm_t, nt_r, TENS), keepdims=True)
     clip = clip_from(square_sum)
 
-    new_param, new_mom, new_vel = adamw_step(p_v[...], m_v[...], v_v[...], clip * gt[0:BLK, :])
+    new_param, new_mom, new_vel = adamw_step(state[0], state[1], state[2], clip * gt[0:BLK, :])
     mine = pl.multiple_of(dp * BLK, BLK)
     wt[pl.ds(mine, BLK), :] = new_param.astype(BF16)
 
@@ -330,11 +328,11 @@
         return gather_copy(fwd_s, own_r, 4 + i, 0, None, WAYS[i][0])
 
     def fwd1_copy(i, half):
-        return gather_copy(fwd_s, fwd_r, 2 * i + half, -2 * WAYS[i][0], half, WAYS[i][0])
+        return gather_copy(fwd_s, fwd_r, half if i == 0 else 1 - half, -2 * WAYS[i][0], half, WAYS[i][0])
 
     def fwd2_copy(i):
         sign, half = WAYS[i]
-        return gather_copy(fwd_s, fwd_r, 4 + i, -2 * sign, half, 2 * sign)
+        return gather_copy(fwd_s, fwd_r, 2, -2 * sign, half, 2 * sign)
 
     def share_copy(off, half):
         rows = rows_of(off, core, half)
@@ -349,7 +347,7 @@
     o_param[...] = new_param
     o_mom[...] = new_mom
     o_vel[...] = new_vel
-    new_cparam, new_cmom, new_cvel = adamw_step(cp_v[...], cm_v[...], cv_v[...], clip * conv_avg)
+    new_cparam, new_cmom, new_cvel = adamw_step(cstate[0], cstate[1], cstate[2], clip * conv_avg)
     o_cparam[...] = new_cparam
     o_cmom[...] = new_cmom
     o_cvel[...] = new_cvel
@@ -387,14 +385,13 @@
 
         lax.fori_loop(0, 3, step, 0)
 
-    for i, (sign, half) in enumerate(WAYS):
-        fwd2_copy(i).wait_recv()
+    landed(wt_rows(2 * HALF), fwd_r.at[2])
+    for i, (_, half) in enumerate(WAYS):
         share_copy(4, half).start()
     for k in range(2):
+        landed(wt_rows(2 * HALF), fwd_r.at[k])
         for i, (sign, half) in enumerate(WAYS):
-            h = half if k == 0 else 1 - half
-            fwd1_copy(i, h).wait_recv()
-            share_copy(-3 * sign, h).start()
+            share_copy(-3 * sign, half if k == 0 else 1 - half).start()
     landed(wt_rows(5 * BLK), share_r.at[0])
     pair = y // 2
     back(2 * pair)
@@ -451,25 +448,21 @@
             pltpu.VMEM((4, HALF, ROWS), BF16),
             pltpu.VMEM((2 * REPS, HALF, ROWS), BF16),
             pltpu.VMEM((D, ROWS), BF16),
-            pltpu.VMEM((BLK, ROWS), F32),
-            pltpu.VMEM((BLK, ROWS), F32),
-            pltpu.VMEM((BLK, ROWS), F32),
+            pltpu.VMEM((3, BLK, ROWS), F32),
             pltpu.VMEM((EROW, D), F32),
             pltpu.VMEM((YS, KCONV, CCOL), F32),
             pltpu.VMEM((2, KCONV, CCOL), F32),
             pltpu.VMEM((REPS, KCONV, CCOL), F32),
-            pltpu.VMEM((KCONV, CCOL), F32),
-            pltpu.VMEM((KCONV, CCOL), F32),
-            pltpu.VMEM((KCONV, CCOL), F32),
+            pltpu.VMEM((3, KCONV, CCOL), F32),
             pltpu.VMEM((2 * YS, 8, 128), F32),
             pltpu.VMEM((TENS, 8, 128), F32),
-            dma((12,)),
+            dma((8,)),
             dma, dma((YS,)),
             dma, dma,
-            dma((2,)), dma((4,)), dma((2,)), dma((2,)),
+            dma((2,)), dma((2,)), dma((2,)),
             dma, dma((2,)),
             dma, dma((6,)),
-            dma, dma((6,)),
+            dma, dma((3,)),
             dma, dma((3,)),
             dma, dma,
             dma, dma,

time: 58.6 us -> 58.5 us (level)
  no operation moved by 1% of the time
where the time goes in v5:
time: 58.5 us; the launch traced here: 58.4 us
  Pallas kernels  57.7 us (99%)
  between operations  0.64 us (1%)
    pallas_call x1, Pallas kernels, body(): pl.pallas_call(kernel, out_shape=(block, block, block, jax.ShapeDtypeStru...  56.5 us
    pallas_call x1, Pallas kernels, body(): pl.pallas_call(hand_over, out_shape=tuple((jax.ShapeDtypeStruct(x.shape,...  1.27 us

profile of v5, /device:TPU:1, one launch (start us, length us, event | category | flops | bytes accessed | tf_op | source)
XLA Modules:
  0.0 58.4 jit_solution(16374054106888037061)
XLA Ops:
  0.6 56.5 %adamw_step.1 = (f32[96,384]{1,0:T(8,128)S(1)}, f32[96,384]{1,0:T(8,128)S(1)}, f32[96,384]{1,0:T(8,128)S(1)}, f32[24,1536]{1,0:T(8,128)S(1)}, bf16[384,1536]{1,0...) custom-call(f32[384,1536]{1,0:T(8,128)} %bitcast.8, f32[4,416]{1,0:T(4,128)} %bitcast.12, ...), custom_call_target="tpu_custom_call" | custom-call | tf_op jit(solution)/shard_map/adamw_step/pallas_call | solution.py:426
  57.1 1.3 %hand_over.1 = (f32[96,384]{1,0:T(8,128)}, f32[96,384]{1,0:T(8,128)}, f32[96,384]{1,0:T(8,128)}, f32[24,1536]{1,0:T(8,128)}, bf16[384,1536]{1,0:T(8,128)(2,1)}, ...) custom-call(f32[96,384]{1,0:T(8,128)S(1)} %get-tuple-element.24.refs_0_, ...), custom_call_target="tpu_custom_call" | custom-call | tf_op jit(solution)/shard_map/hand_over/pallas_call | solution.py:487

commit v6 on v5

--- a/solution.py
+++ b/solution.py
@@ -122,7 +122,6 @@
         late.append(pltpu.make_async_copy(src, dst, load_sem.at[i]))
 
     x_near = [{"tensor": (ten + 2) % TENS}, {"tensor": (ten + TENS - 2) % TENS}, {"tensor": ten + 1 - 2 * (ten % 2)}]
-    z_near = [{"rep": (rep + 1) % REPS}, {"rep": (rep + REPS - 1) % REPS}]
     y_near = [{"dp": 2 * y_at(off) + core} for off in (2, -2, 1, -1)]
     barrier = pltpu.get_barrier_semaphore()
 
@@ -130,7 +129,15 @@
         for device in devices:
             pl.semaphore_signal(sem, inc=1, device_id=device, device_id_type=MESH)
 
-    signal(barrier, y_near[:2] + z_near + y_near[2:] + x_near + [{"dp": partner}])
+    def signal_reps(sem, first, end):
+        def step(i, carry):
+            pl.semaphore_signal(sem, inc=1, device_id={"rep": i}, device_id_type=MESH)
+            return carry
+
+        lax.fori_loop(first, end, step, 0)
+
+    signal(barrier, y_near + x_near + [{"dp": partner}])
+    signal_reps(barrier, rep + 1, REPS)
 
     def turn_group(i):
         loads[i].wait()
@@ -161,14 +168,14 @@
         copy.start()
     for i in range(4):
         turn_group(i)
-    pl.semaphore_wait(barrier, 10)
+    pl.semaphore_wait(barrier, 8 + rep)
     def pair_start(groups):
         for i in groups:
             for k in range(2):
                 pair_copy(2 * order[i] + k).start()
 
     pair_start((0, 1))
-    signal(hello_z, z_near)
+    signal_reps(hello_z, 0, rep)
     signal(hello_x.at[0], x_near)
 
     arrived = set()
@@ -230,7 +237,10 @@
         rel_out[2 * i + h] = encode(total)
         rel_copy(i, h).start()
     conv_load.wait()
-    pl.semaphore_wait(hello_z, 2)
+    @pl.when(rep < REPS - 1)
+    def _():
+        pl.semaphore_wait(hello_z, REPS - 1 - rep)
+
     for off in range(1, REPS):
         conv_z_copy(off).start()
     pl.semaphore_wait(hello_x.at[0], 3)

time: 58.5 us -> 58.6 us (level)
  no operation moved by 1% of the time
where the time goes in v6:
time: 58.6 us; the launch traced here: 58.4 us
  Pallas kernels  57.8 us (99%)
  between operations  0.64 us (1%)
    pallas_call x1, Pallas kernels, body(): pl.pallas_call(kernel, out_shape=(block, block, block, jax.ShapeDtypeStru...  56.5 us
    pallas_call x1, Pallas kernels, body(): pl.pallas_call(hand_over, out_shape=tuple((jax.ShapeDtypeStruct(x.shape,...  1.27 us

profile of v6, /device:TPU:1, one launch (start us, length us, event | category | flops | bytes accessed | tf_op | source)
XLA Modules:
  0.0 58.4 jit_solution(2576749799954480850)
XLA Ops:
  0.6 56.5 %adamw_step.1 = (f32[96,384]{1,0:T(8,128)S(1)}, f32[96,384]{1,0:T(8,128)S(1)}, f32[96,384]{1,0:T(8,128)S(1)}, f32[24,1536]{1,0:T(8,128)S(1)}, bf16[384,1536]{1,0...) custom-call(f32[384,1536]{1,0:T(8,128)} %bitcast.8, f32[4,416]{1,0:T(4,128)} %bitcast.12, ...), custom_call_target="tpu_custom_call" | custom-call | tf_op jit(solution)/shard_map/adamw_step/pallas_call | solution.py:436
  57.1 1.3 %hand_over.1 = (f32[96,384]{1,0:T(8,128)}, f32[96,384]{1,0:T(8,128)}, f32[96,384]{1,0:T(8,128)}, f32[24,1536]{1,0:T(8,128)}, bf16[384,1536]{1,0:T(8,128)(2,1)}, ...) custom-call(f32[96,384]{1,0:T(8,128)S(1)} %get-tuple-element.24.refs_0_, ...), custom_call_target="tpu_custom_call" | custom-call | tf_op jit(solution)/shard_map/hand_over/pallas_call | solution.py:497

commit v7 on v6

--- a/solution.py
+++ b/solution.py
@@ -362,7 +362,6 @@
     o_cmom[...] = new_cmom
     o_cvel[...] = new_cvel
 
-    sent(wt_rows(4 * HALF), own_s)
     for i in range(2):
         own1_copy(i).start()
 
@@ -414,6 +413,7 @@
     row_block = jnp.where(core == 0, near[0:EROW], near[EROW:])
     o_ema[...] = 0.9 * e_v[...] + 0.1 * row_block
 
+    sent(wt_rows(4 * HALF), own_s)
     sent(wt_rows(10 * HALF), fwd_s)
     sent(wt_rows(8 * BLK), share_s)
 

time: 58.6 us -> 58.4 us (level)
  no operation moved by 1% of the time
where the time goes in v7:
time: 58.4 us; the launch traced here: 58.3 us
  Pallas kernels  57.6 us (99%)
  between operations  0.64 us (1%)
    pallas_call x1, Pallas kernels, body(): pl.pallas_call(kernel, out_shape=(block, block, block, jax.ShapeDtypeStru...  56.4 us
    pallas_call x1, Pallas kernels, body(): pl.pallas_call(hand_over, out_shape=tuple((jax.ShapeDtypeStruct(x.shape,...  1.27 us

profile of v7, /device:TPU:1, one launch (start us, length us, event | category | flops | bytes accessed | tf_op | source)
XLA Modules:
  0.0 58.3 jit_solution(13721970689525633319)
XLA Ops:
  0.6 56.4 %adamw_step.1 = (f32[96,384]{1,0:T(8,128)S(1)}, f32[96,384]{1,0:T(8,128)S(1)}, f32[96,384]{1,0:T(8,128)S(1)}, f32[24,1536]{1,0:T(8,128)S(1)}, bf16[384,1536]{1,0...) custom-call(f32[384,1536]{1,0:T(8,128)} %bitcast.8, f32[4,416]{1,0:T(4,128)} %bitcast.12, ...), custom_call_target="tpu_custom_call" | custom-call | tf_op jit(solution)/shard_map/adamw_step/pallas_call | solution.py:436
  57.0 1.3 %hand_over.1 = (f32[96,384]{1,0:T(8,128)}, f32[96,384]{1,0:T(8,128)}, f32[96,384]{1,0:T(8,128)}, f32[24,1536]{1,0:T(8,128)}, bf16[384,1536]{1,0:T(8,128)(2,1)}, ...) custom-call(f32[96,384]{1,0:T(8,128)S(1)} %get-tuple-element.24.refs_0_, ...), custom_call_target="tpu_custom_call" | custom-call | tf_op jit(solution)/shard_map/hand_over/pallas_call | solution.py:497
